TPU v7x, 32 devices: a whole 2x2x4 slice. The times are simulated.
32 devices in a mesh: rep: 4 (over y, x), shard: 8 (over z, core).
Axes of the slice: x: 2, y: 2, z: 4, core: 2. Of those that a mesh axis runs over, the one named last changes fastest.
Arguments:
- tokens: bfloat16 [8192, 1024], P(('rep', 'shard')), may hold values from -6 to 6
- choices: int32 [8192, 8], P(('rep', 'shard')), may hold values from 0 to 31, all different within a row; in each aligned block of 256 rows (0 to 255, 256 to 511, ...) at most 96 rows name the same one
- cont_lengths: int32 [4, 2], P('rep'), may hold values from 1 to 768, 1024 in all within a row
- norm_attn: bfloat16 [1024], P('shard'), may hold values from 0.5 to 1.5
- w_qkv: bfloat16 [1024, 2048], P('shard'), may hold values from -0.1875 to 0.1875
- w_out: bfloat16 [1024, 1024], P('shard'), may hold values from -1.5 to 1.5
- norm_ffn: bfloat16 [1024], P('shard'), may hold values from 0.5 to 1.5
- w_router: bfloat16 [1024, 32], P('shard'), may hold values from -0.25 to 0.25
- w_gate_up: bfloat16 [32, 1024, 1024], P('shard'), may hold values from -0.1875 to 0.1875
- w_down: bfloat16 [32, 512, 1024], P('shard'), may hold values from -0.25 to 0.25
- cotangent: bfloat16 [8192, 1024], P(('rep', 'shard')), may hold values from -6 to 6
Outputs:
- output: bfloat16 [8192, 1024], P(('rep', 'shard'))
- d_tokens: float32 [8192, 1024], P(('rep', 'shard'))
- grad_norm_attn: float32 [1024], P('shard')
- grad_qkv: float32 [1024, 2048], P('shard')
- grad_out: float32 [1024, 1024], P('shard')
- grad_norm_ffn: float32 [1024], P('shard')
- grad_router: float32 [1024, 32], P('shard')
- grad_gate_up: float32 [32, 1024, 1024], P('shard')
- grad_down: float32 [32, 512, 1024], P('shard')
Inputs may be any that keep to these rules, and one draw needn't show every extreme that they name: `choices`: in the rows of one device (aligned blocks of 256 rows) no expert is named by more than 96 rows, a bound that some block reaches; a row names 8 different experts. `cont_lengths`: each row holds the 2 continuation lengths of one group; they sum to 1024 and none is longer than 768.
All inputs are finite; a program needn't handle non-finite values.
Results may differ from a plain program's by a relative error of at most 0.02.
Values may be sent and summed in bfloat16 or wider, within the bound.
A program may use at most 192 MiB of HBM per device.

v0:
```python
import jax
import jax.numpy as jnp
from jax import lax
from jax.sharding import PartitionSpec as P

HEADS = 16
KV_HEADS = 8
HEAD = 64
EXPERTS = 32
FF = 512
TOPK = 8
CAP = 96


EPSILON = 1e-06


def layout(lengths, tok_index, prompt_len):
    starts = prompt_len + jnp.cumsum(lengths) - lengths
    passed = tok_index[:, None] >= starts[None, :]
    segment = jnp.sum(passed.astype(jnp.int32), axis=1)
    seg_start = jnp.max(jnp.where(passed, starts[None, :], 0), axis=1)
    position = jnp.where(segment > 0, tok_index - seg_start + prompt_len, tok_index)
    return (segment, position)


def rotary(field_rows, position, direction):
    half_width = field_rows.shape[-1] // 2
    freq_table = 10000.0 ** (-jnp.arange(half_width, dtype=jnp.float32) / half_width)
    angle_table = direction * position.astype(jnp.float32)[:, None] * freq_table[None, :]
    cosine = jnp.cos(angle_table)[:, None, :]
    sine_part = jnp.sin(angle_table)[:, None, :]
    first_half = field_rows[..., :half_width]
    second_half = field_rows[..., half_width:]
    return jnp.concatenate(
        [
            first_half * cosine - second_half * sine_part,
            second_half * cosine + first_half * sine_part,
        ],
        axis=-1,
    )


def block_scores(queries, query_index, query_segment, key_rot, key_index, key_segment):
    scores = jnp.einsum(
        "qgrd,kgd->grqk", queries, key_rot, preferred_element_type=jnp.float32
    ) * queries.shape[-1] ** (-0.5)
    allowed = (key_index[None, :] <= query_index[:, None]) & (
        (key_segment[None, :] == 0) | (key_segment[None, :] == query_segment[:, None])
    )
    return (jnp.where(allowed, scores, -1e30), allowed)


def on_device(
    tokens,
    choices,
    cont_lengths,
    norm_attn,
    w_qkv,
    w_out,
    norm_ffn,
    w_router,
    w_gate_up,
    w_down,
    cotangent,
):
    row_count = tokens.shape[0]
    model_width = tokens.shape[1]
    shard_count = lax.axis_size("shard")
    group_len = row_count * shard_count
    prompt_len = group_len // 2
    lengths_row = cont_lengths[0]
    tok_index = lax.axis_index("shard") * row_count + jnp.arange(row_count, dtype=jnp.int32)
    segment, position = layout(lengths_row, tok_index, prompt_len)
    gain_attn, full_qkv, full_out, gain_ffn, full_router = (
        lax.all_gather(norm_attn, "shard", axis=0, tiled=True),
        lax.all_gather(w_qkv, "shard", axis=0, tiled=True),
        lax.all_gather(w_out, "shard", axis=0, tiled=True),
        lax.all_gather(norm_ffn, "shard", axis=0, tiled=True),
        lax.all_gather(w_router, "shard", axis=0, tiled=True),
    )
    gain_attn = gain_attn.astype(jnp.float32)
    gain_ffn = gain_ffn.astype(jnp.float32)
    tokens_f = tokens.astype(jnp.float32)
    inv_one = lax.rsqrt(jnp.mean(tokens_f * tokens_f, axis=1, keepdims=True) + EPSILON)
    normed_one = tokens_f * inv_one
    first_in = (normed_one * gain_attn).astype(jnp.bfloat16)
    qkv_rows = jnp.dot(first_in, full_qkv, preferred_element_type=jnp.float32)
    query_width = HEADS * HEAD
    key_width = KV_HEADS * HEAD
    repeat_count = HEADS // KV_HEADS
    score_scale = HEAD ** (-0.5)
    queries = (
        rotary(qkv_rows[:, :query_width].reshape(row_count, HEADS, HEAD), position, 1.0)
        .astype(jnp.bfloat16)
        .reshape(row_count, KV_HEADS, repeat_count, HEAD)
    )
    key_rot = rotary(
        qkv_rows[:, query_width : query_width + key_width].reshape(row_count, KV_HEADS, HEAD),
        position,
        1.0,
    ).astype(jnp.bfloat16)
    values = (
        qkv_rows[:, query_width + key_width :]
        .astype(jnp.bfloat16)
        .reshape(row_count, KV_HEADS, HEAD)
    )
    all_keys, all_values = (
        lax.all_gather(key_rot, "shard", axis=0, tiled=True),
        lax.all_gather(values, "shard", axis=0, tiled=True),
    )
    key_block = min(512, prompt_len)
    blocks = group_len // key_block
    group_index = jnp.arange(group_len, dtype=jnp.int32)
    group_segment, group_position = layout(lengths_row, group_index, prompt_len)
    key_stack = (
        all_keys.reshape(blocks, key_block, KV_HEADS, HEAD),
        all_values.reshape(blocks, key_block, KV_HEADS, HEAD),
        group_index.reshape(blocks, key_block),
        group_segment.reshape(blocks, key_block),
    )
    stat_shape = (KV_HEADS, repeat_count, row_count)

    def stats_step(state_acc, key_piece):
        run_max, run_sum = state_acc
        scores, allowed = block_scores(
            queries, tok_index, segment, key_piece[0], key_piece[2], key_piece[3]
        )
        new_max = jnp.maximum(run_max, jnp.max(scores, axis=-1))
        run_sum = run_sum * jnp.exp(run_max - new_max) + jnp.sum(
            jnp.where(allowed, jnp.exp(scores - new_max[..., None]), 0.0), axis=-1
        )
        return ((new_max, run_sum), None)

    (run_max, run_sum), unused = lax.scan(
        stats_step,
        (jnp.full(stat_shape, -1e30, jnp.float32), jnp.zeros(stat_shape, jnp.float32)),
        key_stack,
    )
    log_total = run_max + jnp.log(run_sum)

    def prob_block(key_piece):
        scores, allowed = block_scores(
            queries, tok_index, segment, key_piece[0], key_piece[2], key_piece[3]
        )
        return jnp.where(allowed, jnp.exp(scores - log_total[..., None]), 0.0)

    def mix_step(total_mix, key_piece):
        prob_f32 = prob_block(key_piece)
        return (
            total_mix
            + jnp.einsum(
                "grqk,kgd->qgrd",
                prob_f32.astype(jnp.bfloat16),
                key_piece[1],
                preferred_element_type=jnp.float32,
            ),
            None,
        )

    mix_f32, unused = lax.scan(
        mix_step, jnp.zeros((row_count, KV_HEADS, repeat_count, HEAD), jnp.float32), key_stack
    )
    mixed_heads = mix_f32.reshape(row_count, query_width).astype(jnp.bfloat16)
    residual = tokens_f + jnp.dot(mixed_heads, full_out, preferred_element_type=jnp.float32)
    inv_two = lax.rsqrt(jnp.mean(residual * residual, axis=1, keepdims=True) + EPSILON)
    normed_two = residual * inv_two
    second_in = (normed_two * gain_ffn).astype(jnp.bfloat16)
    logits = jnp.dot(second_in, full_router, preferred_element_type=jnp.float32)
    expert_ids = jnp.arange(EXPERTS, dtype=jnp.int32)
    select = (choices[:, :, None] == expert_ids[None, None, :]).astype(jnp.float32)
    chosen = jnp.sum(select * logits[:, None, :], axis=2)
    gate_weights = jax.nn.softmax(chosen, axis=-1)
    local_experts = w_down.shape[0]
    flat_choice = choices.reshape(-1)
    pair_count = flat_choice.shape[0]
    onehot = (flat_choice[:, None] == expert_ids[None, :]).astype(jnp.int32)
    slot_rank = jnp.sum((jnp.cumsum(onehot, axis=0) - onehot) * onehot, axis=1)
    slot_place = (
        flat_choice // local_experts * CAP + slot_rank
    ) * local_experts + flat_choice % local_experts
    slot_pair = (
        jnp.full((EXPERTS * CAP,), pair_count, jnp.int32)
        .at[slot_place]
        .set(jnp.arange(pair_count, dtype=jnp.int32))
    )
    padded = jnp.concatenate([second_in, jnp.zeros((1, model_width), jnp.bfloat16)], axis=0)
    send_rows = padded[slot_pair // TOPK].reshape(shard_count, CAP, local_experts, model_width)
    received = lax.all_to_all(send_rows, "shard", split_axis=0, concat_axis=0, tiled=True)
    gate_up = jnp.einsum("nced,edf->ncef", received, w_gate_up, preferred_element_type=jnp.float32)
    hidden = (jax.nn.silu(gate_up[..., :FF]) * gate_up[..., FF:]).astype(jnp.bfloat16)
    expert_out = jnp.einsum(
        "ncef,efd->nced", hidden, w_down, preferred_element_type=jnp.float32
    ).astype(jnp.bfloat16)
    returned = lax.all_to_all(expert_out, "shard", split_axis=0, concat_axis=0, tiled=True).reshape(
        -1, model_width
    )
    pair_out = returned[slot_place].reshape(row_count, TOPK, model_width).astype(jnp.float32)
    output = (residual + jnp.sum(gate_weights[:, :, None] * pair_out, axis=1)).astype(jnp.bfloat16)
    grad_in = cotangent.astype(jnp.float32)
    d_gates = jnp.sum(pair_out * grad_in[:, None, :], axis=2)
    d_pairs = (
        (gate_weights[:, :, None] * grad_in[:, None, :])
        .astype(jnp.bfloat16)
        .reshape(pair_count, model_width)
    )
    d_padded = jnp.concatenate([d_pairs, jnp.zeros((1, model_width), jnp.bfloat16)], axis=0)
    d_send = d_padded[slot_pair].reshape(shard_count, CAP, local_experts, model_width)
    d_received = lax.all_to_all(d_send, "shard", split_axis=0, concat_axis=0, tiled=True)
    gate_up = jnp.einsum("nced,edf->ncef", received, w_gate_up, preferred_element_type=jnp.float32)
    gate_part = gate_up[..., :FF]
    up_part = gate_up[..., FF:]
    sigmoid_gate = jax.nn.sigmoid(gate_part)
    silu_gate = gate_part * sigmoid_gate
    hidden = (silu_gate * up_part).astype(jnp.bfloat16)
    d_hidden = jnp.einsum("nced,efd->ncef", d_received, w_down, preferred_element_type=jnp.float32)
    d_gate_up = jnp.concatenate(
        [
            d_hidden * up_part * sigmoid_gate * (1.0 + gate_part * (1.0 - sigmoid_gate)),
            d_hidden * silu_gate,
        ],
        axis=-1,
    ).astype(jnp.bfloat16)
    grad_down = jnp.einsum("ncef,nced->efd", hidden, d_received, preferred_element_type=jnp.float32)
    grad_gate_up = jnp.einsum(
        "nced,ncef->edf", received, d_gate_up, preferred_element_type=jnp.float32
    )
    d_slots = jnp.einsum(
        "ncef,edf->nced", d_gate_up, w_gate_up, preferred_element_type=jnp.float32
    ).astype(jnp.bfloat16)
    d_back = lax.all_to_all(d_slots, "shard", split_axis=0, concat_axis=0, tiled=True).reshape(
        -1, model_width
    )
    d_second = jnp.sum(
        d_back[slot_place].reshape(row_count, TOPK, model_width).astype(jnp.float32), axis=1
    )
    d_chosen = gate_weights * (d_gates - jnp.sum(gate_weights * d_gates, axis=1, keepdims=True))
    d_logits = jnp.sum(select * d_chosen[:, :, None], axis=1)
    d_second = d_second + jnp.dot(
        d_logits, full_router.astype(jnp.float32).T, precision=lax.Precision.HIGHEST
    )
    grad_router = jnp.dot(
        second_in.astype(jnp.float32).T, d_logits, precision=lax.Precision.HIGHEST
    )
    d_norm_two = d_second * gain_ffn
    grad_ffn = jnp.sum(d_second * normed_two, axis=0)
    d_residual = grad_in + inv_two * (
        d_norm_two - normed_two * jnp.mean(d_norm_two * normed_two, axis=1, keepdims=True)
    )
    d_attn = d_residual.astype(jnp.bfloat16)
    grad_out = jnp.dot(mixed_heads.T, d_attn, preferred_element_type=jnp.float32)
    d_mixed = (
        jnp.dot(d_attn, full_out.T, preferred_element_type=jnp.float32)
        .astype(jnp.bfloat16)
        .reshape(row_count, KV_HEADS, repeat_count, HEAD)
    )

    def delta_step(total_delta, key_piece):
        prob_f32 = prob_block(key_piece)
        d_prob = jnp.einsum(
            "qgrd,kgd->grqk", d_mixed, key_piece[1], preferred_element_type=jnp.float32
        )
        return (total_delta + jnp.sum(prob_f32 * d_prob, axis=-1), None)

    row_delta, unused = lax.scan(delta_step, jnp.zeros(stat_shape, jnp.float32), key_stack)

    def score_grad(key_piece):
        prob_f32 = prob_block(key_piece)
        d_prob = jnp.einsum(
            "qgrd,kgd->grqk", d_mixed, key_piece[1], preferred_element_type=jnp.float32
        )
        return (prob_f32, (prob_f32 * (d_prob - row_delta[..., None])).astype(jnp.bfloat16))

    query_zeros = jnp.zeros((row_count, KV_HEADS, repeat_count, HEAD), jnp.float32)

    def full_step(d_queries, key_piece):
        prob_f32, d_scores = score_grad(key_piece)
        d_queries = (
            d_queries
            + jnp.einsum(
                "grqk,kgd->qgrd", d_scores, key_piece[0], preferred_element_type=jnp.float32
            )
            * score_scale
        )
        key_term = (
            jnp.einsum("grqk,qgrd->kgd", d_scores, queries, preferred_element_type=jnp.float32)
            * score_scale
        )
        value_term = jnp.einsum(
            "grqk,qgrd->kgd",
            prob_f32.astype(jnp.bfloat16),
            d_mixed,
            preferred_element_type=jnp.float32,
        )
        return (d_queries, (key_term, value_term))

    d_queries, block_terms = lax.scan(full_step, query_zeros, key_stack)
    key_terms = block_terms[0].reshape(group_len, key_width)
    value_terms = block_terms[1].reshape(group_len, key_width)
    d_keys, d_values = (
        lax.psum_scatter(
            key_terms.astype(jnp.bfloat16), "shard", scatter_dimension=0, tiled=True
        ).astype(jnp.float32),
        lax.psum_scatter(
            value_terms.astype(jnp.bfloat16), "shard", scatter_dimension=0, tiled=True
        ).astype(jnp.float32),
    )
    d_keys = d_keys.reshape(row_count, KV_HEADS, HEAD)
    d_values = d_values.reshape(row_count, KV_HEADS, HEAD)
    d_query_rows = rotary(d_queries.reshape(row_count, HEADS, HEAD), position, -1.0).reshape(
        row_count, query_width
    )
    d_key_rows = rotary(d_keys, position, -1.0).reshape(row_count, key_width)
    d_qkv = jnp.concatenate(
        [d_query_rows, d_key_rows, d_values.reshape(row_count, key_width)], axis=1
    ).astype(jnp.bfloat16)
    grad_qkv = jnp.dot(first_in.T, d_qkv, preferred_element_type=jnp.float32)
    d_first = jnp.dot(d_qkv, full_qkv.T, preferred_element_type=jnp.float32)
    d_norm_one = d_first * gain_attn
    grad_attn = jnp.sum(d_first * normed_one, axis=0)
    d_tokens = d_residual + inv_one * (
        d_norm_one - normed_one * jnp.mean(d_norm_one * normed_one, axis=1, keepdims=True)
    )
    share_attn, share_qkv, share_out, share_ffn, share_router = (
        lax.psum_scatter(
            grad_attn.astype(jnp.bfloat16), "shard", scatter_dimension=0, tiled=True
        ).astype(jnp.float32),
        lax.psum_scatter(
            grad_qkv.astype(jnp.bfloat16), "shard", scatter_dimension=0, tiled=True
        ).astype(jnp.float32),
        lax.psum_scatter(
            grad_out.astype(jnp.bfloat16), "shard", scatter_dimension=0, tiled=True
        ).astype(jnp.float32),
        lax.psum_scatter(
            grad_ffn.astype(jnp.bfloat16), "shard", scatter_dimension=0, tiled=True
        ).astype(jnp.float32),
        lax.psum_scatter(
            grad_router.astype(jnp.bfloat16), "shard", scatter_dimension=0, tiled=True
        ).astype(jnp.float32),
    )
    share_attn, share_qkv, share_out, share_ffn, share_router, grad_gate_up, grad_down = (
        lax.psum(share_attn.astype(jnp.bfloat16), "rep").astype(jnp.float32),
        lax.psum(share_qkv.astype(jnp.bfloat16), "rep").astype(jnp.float32),
        lax.psum(share_out.astype(jnp.bfloat16), "rep").astype(jnp.float32),
        lax.psum(share_ffn.astype(jnp.bfloat16), "rep").astype(jnp.float32),
        lax.psum(share_router.astype(jnp.bfloat16), "rep").astype(jnp.float32),
        lax.psum(grad_gate_up.astype(jnp.bfloat16), "rep").astype(jnp.float32),
        lax.psum(grad_down.astype(jnp.bfloat16), "rep").astype(jnp.float32),
    )
    return (
        output,
        d_tokens,
        share_attn,
        share_qkv,
        share_out,
        share_ffn,
        share_router,
        grad_gate_up,
        grad_down,
    )


def solution(mesh):
    return jax.shard_map(
        on_device,
        mesh=mesh,
        in_specs=(
            P(("rep", "shard"), None),
            P(("rep", "shard"), None),
            P("rep", None),
            P("shard"),
            P("shard", None),
            P("shard", None),
            P("shard"),
            P("shard", None),
            P("shard", None, None),
            P("shard", None, None),
            P(("rep", "shard"), None),
        ),
        out_specs=(
            P(("rep", "shard"), None),
            P(("rep", "shard"), None),
            P("shard"),
            P("shard", None),
            P("shard", None),
            P("shard"),
            P("shard", None),
            P("shard", None, None),
            P("shard", None, None),
        ),
        check_vma=False,
    )
```

profile of v0, /device:TPU:0, one launch (start us, length us, event | category | flops | bytes accessed | tf_op | source)
XLA Modules:
  0.0 1476.5 jit_solution(884753934744604636)
XLA Ops:
  8.0 13.5 all-gather
  25.3 34.2 %all-gather.7.cloned.1.call-done = bf16[1024,2048]{1,0:T(8,128)(2,1)} async-done(((bf16[128,2048]{1,0:T(8,128)(2,1)}), bf16[1024,2048]{1,0:T(8,128)(2,1)}) %all-gather.7.cloned.1.call-update) | async-done | bytes 4194320 | tf_op jit(solution)/shard_map/all_gather | solution.py:77
  66.8 9.6 all-gather.1
  76.4 9.1 reduce-window.9
  86.4 8.3 scatter_custom_fusion
  98.5 39.1 %while.50 = (s32[]{:T(128)}, f32[8,2,256]{2,1,0:T(2,128)S(1)}, f32[8,2,256]{2,1,0:T(2,128)S(1)}, s32[4,512]{1,0:T(4,128)S(1)}, s32[4,512]{1,0:T(4,128)S(1)}, /*i...) while((s32[]{:T(128)}, f32[8,2,256]{2,1,0:T(2,128)S(1)}, ...), condition=%wide.region_8.9_spmd.clone, body=%wide.region_5.8_spmd.clone.sunk | while | flops 285758208 | bytes 18448520 | solution.py:135
  140.8 21.5 %while.51 = (s32[]{:T(128)}, f32[256,8,2,64]{0,3,2,1:T(8,128)}, bf16[4,512,8,64]{1,3,2,0:T(8,128)(2,1)}, s32[4,512]{1,0:T(4,128)S(1)}, s32[4,512]{1,0:T(4,128)S(...) while((s32[]{:T(128)}, f32[256,8,2,64]{0,3,2,1:T(8,128)}, ...), condition=%wide.region_10.11_spmd.clone, body=%wide.region_9.10_spmd.clone.sunk | while | flops 548406016 | bytes 3966091 | solution.py:161
  146.3 5.1 fusion.218
  151.8 5.1 fusion.218
  157.2 5.1 fusion.218
  169.3 13.9 gather_fusion
  183.2 10.1 reshape.538
  193.3 7.9 copy.147
  201.2 4.9 all-to-all-start
  206.2 144.7 %all_gather.27 = bf16[1024,32]{0,1:T(8,128)(2,1)S(1)} all-gather(bf16[128,32]{0,1:T(8,128)(2,1)S(1)} %copy-done.45), channel_id=1, replica_groups=mesh['rep'=4,'shard'=8] {'shard'}, dimensions={0}, use_global_device_ids=true | all-gather | bytes 73728 | tf_op jit(solution)/shard_map/all_gather | solution.py:80
  354.5 18.6 %gather_fusion.2 = bf16[3072,1024]{1,0:T(8,128)(2,1)} fusion(bf16[2049,1024]{1,0:T(8,128)(2,1)} %concatenate.40, s32[3072]{0:T(1024)S(1)} %get-tuple-element.744), kind=kCustom, calls=%fused_computation.2 | custom fusion | bytes 12595200 | tf_op jit(solution)/shard_map/gather | solution.py:208
  373.1 10.1 reshape.540
  383.2 7.8 copy.152
  395.8 13.9 fusion.103
  409.7 125.0 %all-to-all-done.2 = bf16[8,96,4,1024]{3,1,2,0:T(8,128)(2,1)} async-done(((bf16[8,96,4,1024]{3,1,2,0:T(8,128)(2,1)}), bf16[8,96,4,1024]{3,1,2,0:T(8,128)(2,1)}, u32[]{:S(2)}, u32[]{:S(2)}) %all-to-all-start.2) | async-done | bytes 6291488 | tf_op jit(solution)/shard_map/all_to_all | solution.py:209
  534.7 13.2 fusion.94
  548.0 5.6 convert_bitcast_fusion.1
  561.6 13.0 convert_bitcast_fusion
  574.6 6.6 copy.154
  581.2 119.4 %all-to-all-done.1 = bf16[8,96,4,1024]{3,1,2,0:T(8,128)(2,1)} async-done(((bf16[8,96,4,1024]{3,1,2,0:T(8,128)(2,1)}), bf16[8,96,4,1024]{3,1,2,0:T(8,128)(2,1)}, u32[]{:S(2)}, u32[]{:S(2)}) %all-to-all-start.1) | async-done | bytes 6291488 | tf_op jit(solution)/shard_map/all_to_all | solution.py:195
  700.6 4.8 all-to-all-start.3
  705.7 10.4 copy.150
  716.0 9.7 reshape.539
  725.8 14.5 gather_fusion.1
  740.3 6.1 fusion.86
  746.5 97.8 %all-to-all-done.3 = bf16[8,96,4,1024]{3,1,2,0:T(8,128)(2,1)} async-done(((bf16[8,96,4,1024]{3,1,2,0:T(8,128)(2,1)}), bf16[8,96,4,1024]{3,1,2,0:T(8,128)(2,1)}, u32[]{:S(2)}, u32[]{:S(2)}) %all-to-all-start.3) | async-done | bytes 6291488 | tf_op jit(solution)/shard_map/all_to_all | solution.py:231
  844.3 10.4 copy.155
  854.7 9.7 reshape.541
  864.4 14.8 %gather_fusion.3 = bf16[2048,1024]{1,0:T(8,128)(2,1)} fusion(bf16[3072,1024]{1,0:T(8,128)(2,1)} %reshape.541, s32[2048]{0:T(1024)S(1)} %broadcast_clamp_fusion), kind=kCustom, calls=%fused_computation.3 | custom fusion | bytes 8396800 | tf_op jit(solution)/shard_map/gather | solution.py:235
  879.2 5.6 convert_reduce_fusion
  889.7 27.5 %while.52 = (s32[]{:T(128)}, f32[8,2,256]{2,1,0:T(2,128)S(1)}, s32[4,512]{1,0:T(4,128)S(1)}, s32[4,512]{1,0:T(4,128)S(1)}, s32[256]{0:T(256)S(1)}, /*index=5*/bf...) while((s32[]{:T(128)}, f32[8,2,256]{2,1,0:T(2,128)S(1)}, ...), condition=%wide.region_27.28_spmd.clone, body=%wide.region_25.27_spmd.clone.sunk | while | flops 549982976 | bytes 19235984 | solution.py:265
  917.2 78.9 %while.53 = (s32[]{:T(128)}, f32[256,8,2,64]{0,3,2,1:T(8,128)S(1)}, bf16[4,512,8,64]{1,3,2,0:T(8,128)(2,1)}, bf16[4,512,8,64]{1,3,2,0:T(8,128)(2,1)}, bf16[4,512...) while((s32[]{:T(128)}, f32[256,8,2,64]{0,3,2,1:T(8,128)S(1)}, ...), condition=%wide.region_29.30_spmd.clone, body=%wide.region_28.29_spmd.clone.sunk | while | flops 1368916736 | bytes 129960704 | solution.py:297
  1009.2 26.7 %reduce-scatter.8.cloned.1.call-done = bf16[256,512]{0,1:T(8,128)(2,1)} async-done(((bf16[2048,512]{0,1:T(8,128)(2,1)}), bf16[256,512]{0,1:T(8,128)(2,1)}) %reduce-scatter.8.cloned.1.call-update) | async-done | bytes 262160 | tf_op jit(solution)/shard_map/reduce_scatter | solution.py:301
  1037.1 36.2 %reduce-scatter.10.cloned.1.call-done = bf16[256,512]{0,1:T(8,128)(2,1)} async-done(((bf16[2048,512]{0,1:T(8,128)(2,1)}), bf16[256,512]{0,1:T(8,128)(2,1)}) %reduce-scatter.10.cloned.1.call-update) | async-done | bytes 262160 | tf_op jit(solution)/shard_map/reduce_scatter | solution.py:304
  1077.8 12.9 bitcast_convert_fusion
  1092.0 9.3 bitcast_convert_fusion.1
  1101.3 8.8 reduce-scatter.14.cloned.1.call-done
  1110.1 51.7 %reduce-scatter.12.cloned.1.call-done = bf16[128,2048]{1,0:T(8,128)(2,1)} async-done(((bf16[1024,2048]{1,0:T(8,128)(2,1)}), bf16[128,2048]{1,0:T(8,128)(2,1)}) %reduce-scatter.12.cloned.1.call-update) | async-done | bytes 524304 | tf_op jit(solution)/shard_map/reduce_scatter | solution.py:328
  1163.6 29.4 %reduce-scatter.16.cloned.1.call-done = bf16[128,32]{1,0:T(8,128)(2,1)} async-done(((bf16[1024,32]{1,0:T(8,128)(2,1)}), bf16[128,32]{1,0:T(8,128)(2,1)}) %reduce-scatter.16.cloned.1.call-update) | async-done | bytes 8208
  1197.7 13.8 all-reduce.4
  1211.6 11.3 all-reduce.5
  1225.8 225.5 %all-reduce.9.cloned.1.call-done = (bf16[128,2048]{1,0:T(8,128)(2,1)}, bf16[128,1024]{1,0:T(8,128)(2,1)}, bf16[4,1024,1024]{2,1,0:T(8,128)(2,1)}, bf16[4,512,1024]{2,1,0:T(8,128)(2,1)}) async-done(((bf16[128,2048]{1,0:T(8,128)(2,1)}, bf16[128,1024]{1,0:T(8,128)(2,1)}, bf16[4,1024,1024]{2,1,0:T(8,128)(2,1)}, bf16[4,512,1024]{2,1,0:T(8,128)(2,1)}), (bf16[128,2048]{1,0:T(8,128)(2,1)}, ...) | async-done | bytes 13369360 | tf_op jit(solution)/shard_map/psum | solution.py:343
  1451.3 11.9 convert_element_type.220
  (363 shorter events, 233.6 us)
Async XLA Ops:
  7.2 52.3 %all-gather.7.cloned.1.call-start = ((), (), s32[]{:S(2)}) async-start(), calls=%async_computation.9 | async-start | bytes 4718592 | tf_op jit(solution)/shard_map/all_gather | solution.py:77
  7.9 88.7 %all-gather.11.cloned.1.call-start = ((), (), s32[]{:S(2)}) async-start(), calls=%async_computation.11 | async-start | bytes 2359296 | tf_op jit(solution)/shard_map/all_gather | solution.py:109
  21.5 44.0 %copy-start.40 = (f32[8,1,128]{2,1,0:T(1,128)}, f32[8,1,128]{2,1,0:T(1,128)S(1)}, u32[]{:S(2)}) copy-start(f32[8,1,128]{2,1,0:T(1,128)S(1)} %convert_element_type.225) | copy-start | bytes 12292
  24.3 41.9 %copy-start.33 = (s32[256,8]{0,1:T(8,128)S(1)}, s32[256,8]{0,1:T(8,128)}, u32[]{:S(2)}) copy-start(s32[256,8]{0,1:T(8,128)} %param.20) | copy-start | bytes 24580
  24.4 38.8 %copy-start.46 = (f32[256]{0:T(256)}, f32[256]{0:T(256)S(1)}, u32[]{:S(2)}) copy-start(f32[256]{0:T(256)S(1)} %add_rsqrt_fusion.1) | copy-start | bytes 3076
  59.5 7.3 copy-start.48
  64.6 73.1 %all-gather.9.cloned.1.call-start = ((), (), s32[]{:S(2)}) async-start(), calls=%async_computation.10 | async-start | bytes 2359296 | tf_op jit(solution)/shard_map/all_gather | solution.py:110
  65.5 100.1 %all-gather.13.cloned.1.call-start = ((), (), s32[]{:S(2)}) async-start(), calls=%async_computation.12 | async-start | bytes 2359296 | tf_op jit(solution)/shard_map/all_gather | solution.py:78
  76.4 92.0 %copy-start.34 = (f32[8,1,128]{2,1,0:T(1,128)}, f32[8,1,128]{2,1,0:T(1,128)S(1)}, u32[]{:S(2)}) copy-start(f32[8,1,128]{2,1,0:T(1,128)S(1)} %convert_element_type.226) | copy-start | bytes 12292
  86.4 12.1 copy-start.36
  163.5 4.8 copy-start.1
  163.5 4.9 copy-start.5
  163.5 19.7 %copy-start.22 = (s32[256]{0:T(256)}, s32[256]{0:T(256)S(1)}, u32[]{:S(2)}) copy-start(s32[256]{0:T(256)S(1)} %get-tuple-element.1263) | copy-start | bytes 3076
  163.5 19.7 %copy-start.26 = (s32[4,512]{1,0:T(4,128)}, s32[4,512]{1,0:T(4,128)S(1)}, u32[]{:S(2)}) copy-start(s32[4,512]{1,0:T(4,128)S(1)} %get-tuple-element.1266) | copy-start | bytes 24580
  168.3 14.9 %copy-start.42 = (f32[256]{0:T(256)}, f32[256]{0:T(256)S(1)}, u32[]{:S(2)}) copy-start(f32[256]{0:T(256)S(1)} %add_rsqrt_fusion) | copy-start | bytes 3076
  169.3 181.6 %copy-start.11 = (bf16[256,1024]{1,0:T(8,128)(2,1)}, bf16[256,1024]{1,0:T(8,128)(2,1)S(1)}, u32[]{:S(2)}) copy-start(bf16[256,1024]{1,0:T(8,128)(2,1)S(1)} %multiply_convert_fusion.1) | copy-start | bytes 1572868
  201.2 4.9 copy-start.18
  201.2 5.0 copy-start.45
  201.2 189.8 %all-to-all-start = ((bf16[8,96,4,1024]{3,1,2,0:T(8,128)(2,1)}), bf16[8,96,4,1024]{3,1,2,0:T(8,128)(2,1)}, u32[]{:S(2)}, u32[]{:S(2)}) async-start(bf16[8,96,4,1024]{3,1,2,0:T(8,128)(2,1)} %copy.147), calls=%async_computation | async-start | bytes 12582912 | tf_op jit(solution)/shard_map/all_to_all | solution.py:189
  391.0 143.7 %all-to-all-start.2 = ((bf16[8,96,4,1024]{3,1,2,0:T(8,128)(2,1)}), bf16[8,96,4,1024]{3,1,2,0:T(8,128)(2,1)}, u32[]{:S(2)}, u32[]{:S(2)}) async-start(bf16[8,96,4,1024]{3,1,2,0:T(8,128)(2,1)} %copy.152), calls=%async_computation.2 | async-start | bytes 12582912 | tf_op jit(solution)/shard_map/all_to_all | solution.py:209
  534.7 13.2 copy-start.49
  556.8 143.7 %all-to-all-start.1 = ((bf16[8,96,4,1024]{3,1,2,0:T(8,128)(2,1)}), bf16[8,96,4,1024]{3,1,2,0:T(8,128)(2,1)}, u32[]{:S(2)}, u32[]{:S(2)}) async-start(bf16[8,96,4,1024]{3,1,2,0:T(8,128)(2,1)} %copy.149), calls=%async_computation.1 | async-start | bytes 12582912 | tf_op jit(solution)/shard_map/all_to_all | solution.py:195
  581.2 124.4 %copy-start.37 = (s32[2048,1]{0,1:T(1,128)S(1)}, s32[2048,1]{0,1:T(1,128)}, u32[]{:S(2)}) copy-start(s32[2048,1]{0,1:T(1,128)} %copy-done.36) | copy-start | bytes 24580
  700.6 143.8 %all-to-all-start.3 = ((bf16[8,96,4,1024]{3,1,2,0:T(8,128)(2,1)}), bf16[8,96,4,1024]{3,1,2,0:T(8,128)(2,1)}, u32[]{:S(2)}, u32[]{:S(2)}) async-start(bf16[8,96,4,1024]{3,1,2,0:T(8,128)(2,1)} %copy.154), calls=%async_computation.3 | async-start | bytes 12582912 | tf_op jit(solution)/shard_map/all_to_all | solution.py:231
  705.4 330.6 %reduce-scatter.8.cloned.1.call-start = ((), (), s32[]{:S(2)}) async-start(), calls=%async_computation.13 | async-start | bytes 2359296 | tf_op jit(solution)/shard_map/reduce_scatter | solution.py:301
  746.5 138.3 %copy-start.24 = (f32[256,32]{0,1:T(8,128)}, f32[256,32]{0,1:T(8,128)S(1)}, u32[]{:S(2)}) copy-start(f32[256,32]{0,1:T(8,128)S(1)} %select_reduce_fusion.1) | copy-start | bytes 98308
  864.4 20.5 %copy-start.7 = (f32[256,1024]{1,0:T(8,128)S(1)}, f32[256,1024]{1,0:T(8,128)}, u32[]{:S(2)}) copy-start(f32[256,1024]{1,0:T(8,128)} %copy-done.6) | copy-start | bytes 3145732
  864.4 20.5 %copy-start.35 = (f32[8,1,128]{2,1,0:T(1,128)S(1)}, f32[8,1,128]{2,1,0:T(1,128)}, u32[]{:S(2)}) copy-start(f32[8,1,128]{2,1,0:T(1,128)} %copy-done.34) | copy-start | bytes 12292
  864.4 20.5 %copy-start.43 = (f32[256]{0:T(256)S(1)}, f32[256]{0:T(256)}, u32[]{:S(2)}) copy-start(f32[256]{0:T(256)} %copy-done.42) | copy-start | bytes 3076
  879.2 7.3 copy-start.17
  879.2 7.3 copy-start.19
  879.2 9.4 copy-start.10
  929.2 4.8 copy-start.4
  1001.2 5.5 copy-start.9
  1001.2 5.5 copy-start.14
  1001.3 72.0 %reduce-scatter.10.cloned.1.call-start = ((), (), s32[]{:S(2)}) async-start(), calls=%async_computation.14 | async-start | bytes 2359296 | tf_op jit(solution)/shard_map/reduce_scatter | solution.py:304
  1006.6 66.7 %copy-start.15 = (bf16[256,1024]{1,0:T(8,128)(2,1)S(1)}, bf16[256,1024]{1,0:T(8,128)(2,1)}, u32[]{:S(2)}) copy-start(bf16[256,1024]{1,0:T(8,128)(2,1)} %param.19) | copy-start | bytes 1572868
  1006.6 66.7 %copy-start.41 = (f32[8,1,128]{2,1,0:T(1,128)S(1)}, f32[8,1,128]{2,1,0:T(1,128)}, u32[]{:S(2)}) copy-start(f32[8,1,128]{2,1,0:T(1,128)} %copy-done.40) | copy-start | bytes 12292
  1006.6 66.7 %copy-start.47 = (f32[256]{0:T(256)S(1)}, f32[256]{0:T(256)}, u32[]{:S(2)}) copy-start(f32[256]{0:T(256)} %copy-done.46) | copy-start | bytes 3076
  1006.6 103.4 %reduce-scatter.14.cloned.1.call-start = ((), (), s32[]{:S(2)}) async-start(), calls=%async_computation.16 | async-start | bytes 2359296 | tf_op jit(solution)/shard_map/reduce_scatter | solution.py:331
  1008.8 152.9 %reduce-scatter.12.cloned.1.call-start = ((), (), s32[]{:S(2)}) async-start(), calls=%async_computation.15 | async-start | bytes 4718592 | tf_op jit(solution)/shard_map/reduce_scatter | solution.py:328
  1077.8 13.0 copy-start.12
  1077.8 13.0 copy-start.25
  1077.8 115.3 %reduce-scatter.16.cloned.1.call-start = ((), (), s32[]{:S(2)}) async-start(), calls=%async_computation.17 | async-start | bytes 294912
  1092.0 359.3 %all-reduce.9.cloned.1.call-start = ((), (), s32[]{:S(2)}) async-start(), calls=%async_computation.18 | async-start | bytes 26738688 | tf_op jit(solution)/shard_map/psum | solution.py:343
  1161.8 35.9 %copy-start.44 = (bf16[1024]{0:T(1024)(128)(2,1)S(1)}, bf16[1024]{0:T(1024)(128)(2,1)}, u32[]{:S(2)}) copy-start(bf16[1024]{0:T(1024)(128)(2,1)} %get-tuple-element.616) | copy-start | bytes 6148
  1451.3 11.9 copy-start.16
  1463.1 5.5 copy-start.32
  (26 other events, 87.7 us)
Sparse Core Ops, SparseCore 0:
  9.6 49.8 all-gather.6
  64.7 29.5 all-gather.10
  96.5 29.8 all-gather.8
  127.9 28.1 all-gather.12
  1001.4 34.5 reduce-scatter.7
  1038.7 34.5 reduce-scatter.9
  1075.6 34.4 reduce-scatter.13
  1112.9 48.7 reduce-scatter.11
  1164.6 28.4 reduce-scatter.15
  1198.0 253.2 all-reduce.8
where the time goes:
time: 1480 us
  waiting for transfers between devices  756 us (51%)
  matrix products  215 us (15%)
  local copies, waits for them, and re-layouts  198 us (13%)
  blocking collectives  193 us (13%)
  other arithmetic  76.8 us (5%)
  starting transfers between devices  20 us (1%)
  between operations  16 us (1%)
    psum x1, waiting for transfers between devices, on_device(): lax.psum(share_qkv.astype(jnp.bfloat16), 'rep').astype(jnp.float32)  225 us
    all_gather x1, blocking collectives, on_device(): lax.all_gather(w_router, 'shard', axis=0, tiled=True)  145 us
    all_to_all x1, waiting for transfers between devices, on_device(): lax.all_to_all(d_send, 'shard', split_axis=0, concat_axis=0, tiled=True)  125 us
    all_to_all x1, waiting for transfers between devices, on_device(): lax.all_to_all(expert_out, 'shard', split_axis=0, concat_axis=0, tiled=True)  119 us
    all_to_all x1, waiting for transfers between devices, on_device(): lax.all_to_all(d_slots, 'shard', split_axis=0, concat_axis=0, tiled=True)  97.8 us
    reduce_scatter x1, waiting for transfers between devices, on_device(): lax.psum_scatter(grad_qkv.astype(jnp.bfloat16), 'shard', scatter_dimensio...  51.7 us
    dot_general x12, matrix products, block_scores(): jnp.einsum('qgrd,kgd->grqk', queries, key_rot, preferred_element_type=jnp...  37.7 us
    reduce_scatter x1, waiting for transfers between devices, on_device(): lax.psum_scatter(value_terms.astype(jnp.bfloat16), 'shard', scatter_dimen...  36.2 us
  transfers between devices with their start and end apart: 14, of which 10 were waited for; matrix products, arithmetic and copies ran while one was open for 17% of the time, Pallas kernels for 0%

commit v1 on v0

--- a/solution.py
+++ b/solution.py
@@ -16,7 +16,8 @@
 
 
 def layout(lengths, tok_index, prompt_len):
-    starts = prompt_len + jnp.cumsum(lengths) - lengths
+    order = jnp.arange(lengths.shape[0])
+    starts = prompt_len + jnp.sum(jnp.where(order[None, :] < order[:, None], lengths[None, :], 0), axis=1)
     passed = tok_index[:, None] >= starts[None, :]
     segment = jnp.sum(passed.astype(jnp.int32), axis=1)
     seg_start = jnp.max(jnp.where(passed, starts[None, :], 0), axis=1)
@@ -49,6 +50,12 @@
         (key_segment[None, :] == 0) | (key_segment[None, :] == query_segment[:, None])
     )
     return (jnp.where(allowed, scores, -1e30), allowed)
+
+
+def gate_table(logits, named):
+    masked = jnp.where(named, logits, -1e30)
+    weight = jnp.where(named, jnp.exp(masked - jnp.max(masked, axis=1, keepdims=True)), 0.0)
+    return weight / jnp.sum(weight, axis=1, keepdims=True)
 
 
 def on_device(
@@ -167,53 +174,81 @@
     normed_two = residual * inv_two
     second_in = (normed_two * gain_ffn).astype(jnp.bfloat16)
     logits = jnp.dot(second_in, full_router, preferred_element_type=jnp.float32)
+    local_experts = w_down.shape[0]
     expert_ids = jnp.arange(EXPERTS, dtype=jnp.int32)
-    select = (choices[:, :, None] == expert_ids[None, None, :]).astype(jnp.float32)
-    chosen = jnp.sum(select * logits[:, None, :], axis=2)
-    gate_weights = jax.nn.softmax(chosen, axis=-1)
-    local_experts = w_down.shape[0]
-    flat_choice = choices.reshape(-1)
-    pair_count = flat_choice.shape[0]
-    onehot = (flat_choice[:, None] == expert_ids[None, :]).astype(jnp.int32)
-    slot_rank = jnp.sum((jnp.cumsum(onehot, axis=0) - onehot) * onehot, axis=1)
-    slot_place = (
-        flat_choice // local_experts * CAP + slot_rank
-    ) * local_experts + flat_choice % local_experts
-    slot_pair = (
-        jnp.full((EXPERTS * CAP,), pair_count, jnp.int32)
-        .at[slot_place]
-        .set(jnp.arange(pair_count, dtype=jnp.int32))
-    )
-    padded = jnp.concatenate([second_in, jnp.zeros((1, model_width), jnp.bfloat16)], axis=0)
-    send_rows = padded[slot_pair // TOPK].reshape(shard_count, CAP, local_experts, model_width)
-    received = lax.all_to_all(send_rows, "shard", split_axis=0, concat_axis=0, tiled=True)
-    gate_up = jnp.einsum("nced,edf->ncef", received, w_gate_up, preferred_element_type=jnp.float32)
-    hidden = (jax.nn.silu(gate_up[..., :FF]) * gate_up[..., FF:]).astype(jnp.bfloat16)
-    expert_out = jnp.einsum(
-        "ncef,efd->nced", hidden, w_down, preferred_element_type=jnp.float32
+    local_ids = lax.axis_index("shard") * local_experts + jnp.arange(local_experts, dtype=jnp.int32)
+    group_in = lax.all_gather(second_in, "shard", axis=0, tiled=True)
+    group_cot = lax.all_gather(cotangent, "shard", axis=0, tiled=True)
+    group_choice = lax.all_gather(choices, "shard", axis=0, tiled=True)
+    named = jnp.any(choices[:, :, None] == expert_ids[None, None, :], axis=1)
+    gates = gate_table(logits, named)
+    group_named = jnp.any(group_choice[:, :, None] == expert_ids[None, None, :], axis=1)
+    group_logits = jnp.dot(group_in, full_router, preferred_element_type=jnp.float32)
+    group_gates = gate_table(group_logits, group_named)
+    own = (expert_ids[:, None] == local_ids[None, :]).astype(jnp.float32)
+    own_gates = jnp.sum(group_gates[:, :, None] * own[None], axis=1).reshape(
+        shard_count, row_count, local_experts
+    )
+    own_named = jnp.sum(group_named.astype(jnp.float32)[:, :, None] * own[None], axis=1).reshape(
+        shard_count, row_count, local_experts
+    )
+    earlier = (
+        jnp.arange(row_count)[:, None] > jnp.arange(row_count)[None, :]
     ).astype(jnp.bfloat16)
-    returned = lax.all_to_all(expert_out, "shard", split_axis=0, concat_axis=0, tiled=True).reshape(
-        -1, model_width
-    )
-    pair_out = returned[slot_place].reshape(row_count, TOPK, model_width).astype(jnp.float32)
-    output = (residual + jnp.sum(gate_weights[:, :, None] * pair_out, axis=1)).astype(jnp.bfloat16)
-    grad_in = cotangent.astype(jnp.float32)
-    d_gates = jnp.sum(pair_out * grad_in[:, None, :], axis=2)
-    d_pairs = (
-        (gate_weights[:, :, None] * grad_in[:, None, :])
+    rank = jnp.einsum(
+        "st,nte->nse", earlier, own_named.astype(jnp.bfloat16), preferred_element_type=jnp.float32
+    )
+    rank = jnp.where(own_named > 0, rank, -1.0)
+    hit = rank.transpose(0, 2, 1)[:, :, None, :] == jnp.arange(CAP, dtype=jnp.float32)[
+        None, None, :, None
+    ]
+    pick = hit.astype(jnp.bfloat16)
+    slot_gates = jnp.sum(
+        jnp.where(hit, own_gates.transpose(0, 2, 1)[:, :, None, :], 0.0), axis=3
+    ).transpose(1, 0, 2)
+    group_in = group_in.reshape(shard_count, row_count, model_width)
+    group_cot = group_cot.reshape(shard_count, row_count, model_width)
+    slots = shard_count * CAP
+    received = (
+        jnp.einsum("nest,ntd->ensd", pick, group_in, preferred_element_type=jnp.float32)
         .astype(jnp.bfloat16)
-        .reshape(pair_count, model_width)
-    )
-    d_padded = jnp.concatenate([d_pairs, jnp.zeros((1, model_width), jnp.bfloat16)], axis=0)
-    d_send = d_padded[slot_pair].reshape(shard_count, CAP, local_experts, model_width)
-    d_received = lax.all_to_all(d_send, "shard", split_axis=0, concat_axis=0, tiled=True)
-    gate_up = jnp.einsum("nced,edf->ncef", received, w_gate_up, preferred_element_type=jnp.float32)
+        .reshape(local_experts, slots, model_width)
+    )
+    slot_cot = jnp.einsum(
+        "nest,ntd->ensd", pick, group_cot, preferred_element_type=jnp.float32
+    ).reshape(local_experts, slots, model_width)
+    slot_gates = slot_gates.reshape(local_experts, slots)
+    d_received = (slot_cot * slot_gates[:, :, None]).astype(jnp.bfloat16)
+    gate_up = jnp.einsum("ecd,edf->ecf", received, w_gate_up, preferred_element_type=jnp.float32)
     gate_part = gate_up[..., :FF]
     up_part = gate_up[..., FF:]
     sigmoid_gate = jax.nn.sigmoid(gate_part)
     silu_gate = gate_part * sigmoid_gate
     hidden = (silu_gate * up_part).astype(jnp.bfloat16)
-    d_hidden = jnp.einsum("nced,efd->ncef", d_received, w_down, preferred_element_type=jnp.float32)
+    expert_out = jnp.einsum("ecf,efd->ecd", hidden, w_down, preferred_element_type=jnp.float32)
+    scaled_out = (expert_out * slot_gates[:, :, None]).astype(jnp.bfloat16)
+    slot_d_gates = jnp.sum(expert_out * slot_cot, axis=2)
+    out_terms = jnp.einsum(
+        "nest,ensd->ntd",
+        pick,
+        scaled_out.reshape(local_experts, shard_count, CAP, model_width),
+        preferred_element_type=jnp.float32,
+    ).reshape(group_len, model_width)
+    pair_sum = lax.psum_scatter(
+        out_terms.astype(jnp.bfloat16), "shard", scatter_dimension=0, tiled=True
+    ).astype(jnp.float32)
+    output = (residual + pair_sum).astype(jnp.bfloat16)
+    grad_in = cotangent.astype(jnp.float32)
+    own_d_gates = jnp.sum(
+        jnp.where(
+            hit, slot_d_gates.reshape(local_experts, shard_count, CAP).transpose(1, 0, 2)[..., None], 0.0
+        ),
+        axis=2,
+    ).transpose(0, 2, 1)
+    d_gates = lax.all_to_all(
+        own_d_gates.reshape(group_len, local_experts), "shard", split_axis=0, concat_axis=1, tiled=True
+    )
+    d_hidden = jnp.einsum("ecd,efd->ecf", d_received, w_down, preferred_element_type=jnp.float32)
     d_gate_up = jnp.concatenate(
         [
             d_hidden * up_part * sigmoid_gate * (1.0 + gate_part * (1.0 - sigmoid_gate)),
@@ -221,21 +256,21 @@
         ],
         axis=-1,
     ).astype(jnp.bfloat16)
-    grad_down = jnp.einsum("ncef,nced->efd", hidden, d_received, preferred_element_type=jnp.float32)
-    grad_gate_up = jnp.einsum(
-        "nced,ncef->edf", received, d_gate_up, preferred_element_type=jnp.float32
-    )
+    grad_down = jnp.einsum("ecf,ecd->efd", hidden, d_received, preferred_element_type=jnp.float32)
+    grad_gate_up = jnp.einsum("ecd,ecf->edf", received, d_gate_up, preferred_element_type=jnp.float32)
     d_slots = jnp.einsum(
-        "ncef,edf->nced", d_gate_up, w_gate_up, preferred_element_type=jnp.float32
+        "ecf,edf->ecd", d_gate_up, w_gate_up, preferred_element_type=jnp.float32
     ).astype(jnp.bfloat16)
-    d_back = lax.all_to_all(d_slots, "shard", split_axis=0, concat_axis=0, tiled=True).reshape(
-        -1, model_width
-    )
-    d_second = jnp.sum(
-        d_back[slot_place].reshape(row_count, TOPK, model_width).astype(jnp.float32), axis=1
-    )
-    d_chosen = gate_weights * (d_gates - jnp.sum(gate_weights * d_gates, axis=1, keepdims=True))
-    d_logits = jnp.sum(select * d_chosen[:, :, None], axis=1)
+    d_terms = jnp.einsum(
+        "nest,ensd->ntd",
+        pick,
+        d_slots.reshape(local_experts, shard_count, CAP, model_width),
+        preferred_element_type=jnp.float32,
+    ).reshape(group_len, model_width)
+    d_second = lax.psum_scatter(
+        d_terms.astype(jnp.bfloat16), "shard", scatter_dimension=0, tiled=True
+    ).astype(jnp.float32)
+    d_logits = gates * (d_gates - jnp.sum(gates * d_gates, axis=1, keepdims=True))
     d_second = d_second + jnp.dot(
         d_logits, full_router.astype(jnp.float32).T, precision=lax.Precision.HIGHEST
     )

time: 1480 us -> 1040 us (0.70)
  waiting for transfers between devices: 756 us -> 555 us
  local copies, waits for them, and re-layouts: 198 us -> 56.5 us
  blocking collectives: 193 us -> 75.7 us
  matrix products: 215 us -> 249 us
  starting transfers between devices: 20 us -> 4.63 us
    all_to_all x4 -> x1, waiting for transfers between devices: 342 us -> 6.08 us  [on_device(): lax.all_to_all(own_d_gates.reshape(group_len, local_experts), 'shard', sp...]
    all_gather x1, blocking collectives: 145 us -> 13.6 us  [on_device(): lax.all_gather(w_router, 'shard', axis=0, tiled=True)]
    reduce_scatter x0 -> x2, waiting for transfers between devices: none -> 79.4 us  [the longest x1 47.5 us: on_device(): lax.psum_scatter(out_terms.astype(jnp.bfloat16), 'shard', scatter_dimensi...]
    gather x4 -> x0, local copies, waits for them, and re-layouts: 61.8 us -> none  [the longest x1 18.6 us: on_device(): d_padded[slot_pair].reshape(shard_count, CAP, local_experts, model_width)]
    reshape x7 -> x1, local copies, waits for them, and re-layouts: 55.3 us -> 0.08 us  [on_device(): slot_d_gates.reshape(local_experts, shard_count, CAP).transpose(1, 0, 2)]
    all_gather x0 -> x2, waiting for transfers between devices: none -> 38.5 us  [the longest x1 20.8 us: on_device(): group_cot = lax.all_gather(cotangent, 'shard', axis=0, tiled=True)]
    dot_general x6 -> x12, matrix products: 67.9 us -> 97.5 us  [the longest x1 13.6 us: on_device(): jnp.einsum('ecf,edf->ecd', d_gate_up, w_gate_up, preferred_element_type=j...]
    all_to_all x2 -> x1, local copies, waits for them, and re-layouts: 20.7 us -> 0.01 us  [on_device(): lax.all_to_all(own_d_gates.reshape(group_len, local_experts), 'shard', sp...]
  transfers between devices with their start and end apart: 14 -> 15, of which waited for: 10 -> 13; matrix products, arithmetic and copies ran while one was open for 17% -> 15% of each run, Pallas kernels for 0% -> 0%
where the time goes in v1:
time: 1040 us
  waiting for transfers between devices  555 us (53%)
  matrix products  249 us (24%)
  other arithmetic  77.1 us (7%)
  blocking collectives  75.7 us (7%)
  local copies, waits for them, and re-layouts  56.5 us (5%)
  between operations  15.7 us (2%)
    psum x1, waiting for transfers between devices, on_device(): lax.psum(share_qkv.astype(jnp.bfloat16), 'rep').astype(jnp.float32)  226 us
    reduce_scatter x1, waiting for transfers between devices, on_device(): lax.psum_scatter(grad_qkv.astype(jnp.bfloat16), 'shard', scatter_dimensio...  51.2 us
    reduce_scatter x1, waiting for transfers between devices, on_device(): lax.psum_scatter(out_terms.astype(jnp.bfloat16), 'shard', scatter_dimensi...  47.5 us
    dot_general x12, matrix products, block_scores(): jnp.einsum('qgrd,kgd->grqk', queries, key_rot, preferred_element_type=jnp...  37.7 us
    reduce_scatter x1, waiting for transfers between devices, on_device(): lax.psum_scatter(value_terms.astype(jnp.bfloat16), 'shard', scatter_dimen...  36.2 us
    all_gather x1, waiting for transfers between devices, on_device(): lax.all_gather(w_qkv, 'shard', axis=0, tiled=True)  34.9 us
    reduce_scatter x1, waiting for transfers between devices, on_device(): lax.psum_scatter(d_terms.astype(jnp.bfloat16), 'shard', scatter_dimension...  31.8 us
    unnamed x15, waiting for transfers between devices  31.4 us
  transfers between devices with their start and end apart: 15, of which 13 were waited for; matrix products, arithmetic and copies ran while one was open for 15% of the time, Pallas kernels for 0%

profile of v1, /device:TPU:0, one launch (start us, length us, event | category | flops | bytes accessed | tf_op | source)
XLA Modules:
  0.0 1035.3 jit_solution(11300766700973344985)
XLA Ops:
  8.0 13.5 %all-gather = bf16[8,1,128]{2,1,0:T(2,128)(2,1)S(1)} all-gather(bf16[1,1,128]{2,1,0:T(2,128)(2,1)} %bitcast.420), channel_id=1, replica_groups=mesh['rep'=4,'shard'=8] {'shard'}, dimensions={0}, use_global_device_ids=true | all-gather | bytes 2304 | tf_op jit(solution)/shard_map/all_gather | solution.py:83
  24.6 34.9 %all-gather.9.cloned.1.call-done = bf16[1024,2048]{1,0:T(8,128)(2,1)} async-done(((bf16[128,2048]{1,0:T(8,128)(2,1)}), bf16[1024,2048]{1,0:T(8,128)(2,1)}) %all-gather.9.cloned.1.call-update) | async-done | bytes 4194320 | tf_op jit(solution)/shard_map/all_gather | solution.py:84
  66.3 9.6 all-gather.1
  77.7 16.5 %all-gather.13.cloned.1.call-done = bf16[2048,8,64]{0,2,1:T(8,128)(2,1)} async-done(((bf16[256,8,64]{0,2,1:T(8,128)(2,1)}), bf16[2048,8,64]{0,2,1:T(8,128)(2,1)}) %all-gather.13.cloned.1.call-update) | async-done | bytes 2097168 | tf_op jit(solution)/shard_map/all_gather | solution.py:116
  96.1 39.2 %while.50 = (s32[]{:T(128)}, f32[8,2,256]{2,1,0:T(2,128)S(1)}, f32[8,2,256]{2,1,0:T(2,128)S(1)}, s32[4,512]{1,0:T(4,128)S(1)}, s32[4,512]{1,0:T(4,128)S(1)}, /*i...) while((s32[]{:T(128)}, f32[8,2,256]{2,1,0:T(2,128)S(1)}, ...), condition=%wide.region_8.9_spmd.clone, body=%wide.region_5.8_spmd.clone.sunk | while | flops 285758208 | bytes 18448520 | solution.py:142
  96.5 4.8 fusion.212
  101.2 4.8 select_reduce_fusion.4
  106.4 4.8 fusion.212
  116.2 4.8 fusion.212
  125.9 4.8 fusion.212
  138.6 21.6 %while.51 = (s32[]{:T(128)}, f32[256,8,2,64]{0,3,2,1:T(8,128)}, bf16[4,512,8,64]{1,3,2,0:T(8,128)(2,1)}, s32[4,512]{1,0:T(4,128)S(1)}, s32[4,512]{1,0:T(4,128)S(...) while((s32[]{:T(128)}, f32[256,8,2,64]{0,3,2,1:T(8,128)}, ...), condition=%wide.region_10.11_spmd.clone, body=%wide.region_9.10_spmd.clone.sunk | while | flops 548406016 | bytes 3966091 | solution.py:168
  138.9 4.8 fusion.219
  144.1 5.2 fusion.219
  149.6 5.1 fusion.219
  155.0 5.1 fusion.219
  168.7 14.1 %all_gather.35 = s32[2048,8]{0,1:T(8,128)S(1)} all-gather(s32[256,8]{0,1:T(8,128)S(1)} %copy-done.38), channel_id=1, replica_groups=mesh['rep'=4,'shard'=8] {'shard'}, dimensions={0}, use_global_device_ids=true | all-gather | bytes 73728 | tf_op jit(solution)/shard_map/all_gather | solution.py:182
  183.1 13.6 %all_gather.38 = bf16[1024,32]{0,1:T(8,128)(2,1)S(1)} all-gather(bf16[128,32]{0,1:T(8,128)(2,1)} %param.26), channel_id=1, replica_groups=mesh['rep'=4,'shard'=8] {'shard'}, dimensions={0}, use_global_device_ids=true | all-gather | bytes 73728 | tf_op jit(solution)/shard_map/all_gather | solution.py:87
  197.4 17.8 %all-gather.17.cloned.1.call-done = bf16[2048,1024]{1,0:T(8,128)(2,1)} async-done(((bf16[256,1024]{1,0:T(8,128)(2,1)}), bf16[2048,1024]{1,0:T(8,128)(2,1)}) %all-gather.17.cloned.1.call-update) | async-done | bytes 4194320 | tf_op jit(solution)/shard_map/all_gather | solution.py:180
  222.6 11.4 %fusion.146 = f32[4,768,1024]{2,1,0:T(8,128)S(1)} fusion(bf16[4,768,1024]{2,1,0:T(8,128)(2,1)S(1)} %bitcast.373, bf16[4,1024,1024]{2,1,0:T(8,128)(2,1)} %param.27), kind=kOutput, calls=%fused_computation.232 | convolution fusion | flops 6442450944 | bytes 27262976 | tf_op jit(solution)/shard_map/ecd,edf->ecf/dot_general | solution.py:222
  241.7 20.8 %all-gather.19.cloned.1.call-done = bf16[2048,1024]{1,0:T(8,128)(2,1)} async-done(((bf16[256,1024]{1,0:T(8,128)(2,1)}), bf16[2048,1024]{1,0:T(8,128)(2,1)}) %all-gather.19.cloned.1.call-update) | async-done | bytes 4194320 | tf_op jit(solution)/shard_map/all_gather | solution.py:181
  262.5 8.8 convolution_bitcast_fusion.1
  271.3 12.0 %copy.157 = f32[4,8,96,1024]{3,2,1,0:T(8,128)} copy(f32[4,8,96,1024]{3,2,0,1:T(8,128)} %convolution_bitcast_fusion.1) | data formatting | bytes 25165824 | tf_op jit(solution)/shard_map/nest,ntd->ensd/transpose | solution.py:217
  283.2 10.7 %fusion.86 = (f32[4,768]{1,0:T(4,128)S(1)}, f32[4,768,1024]{2,1,0:T(8,128)}) fusion(f32[4,8,96,1024]{3,2,1,0:T(8,128)} %copy.157, bf16[4,768,512]{2,1,0:T(8,128)(2,1)S(1)} %copy-done.5, bf16[4,512,1024]{2,1,0:T(8,128)(2,1)} %param.28), kind=kOutput, calls=%fused_computation.102 | convolution fusion | flops 3227513856 | bytes 32518144 | tf_op jit(solution)/shard_map/ecf,efd->ecd/dot_general | solution.py:228
  296.0 14.1 %fusion.85 = (bf16[4,768,1024]{2,1,0:T(8,128)(2,1)}, bf16[4,768,1024]{2,1,0:T(8,128)(2,1)}) fusion(f32[4,8,96,1024]{3,2,1,0:T(8,128)} %copy.157, f32[4,768]{1,0:T(4,128)S(1)} %mul.420, f32[4,768,1024]{2,1,0:T(8,128)} %get-tuple-element.758), kind=kLoop, calls=%fused_computation.101 | loop fusion | flops 12582912 | bytes 37761024 | tf_op jit(solution)/shard_map/convert_element_type | solution.py:221
  310.1 12.0 %multiply_convert_fusion.2 = (bf16[4,768,512]{2,1,0:T(8,128)(2,1)S(1)}, bf16[4,768,512]{2,1,0:T(8,128)(2,1)}) fusion(f32[4,768,1024]{2,1,0:T(8,128)} %copy-done.11, bf16[4,768,1024]{2,1,0:T(8,128)(2,1)} %get-tuple-element.745, bf16[4,512,1024]{2,1,0:T(8,128)(2,1)S(1)} %copy-done.12), kind=kOutput, calls=%fused_computation.113 | convolution fusion | flops 3241672704 | bytes 29360128 | tf_op jit(solution)/shard_map/ecd,efd->ecf/dot_general | solution.py:251
  322.1 13.6 %fusion.93 = bf16[4,768,1024]{2,1,0:T(8,128)(2,1)} fusion(bf16[4,1024,1024]{2,1,0:T(8,128)(2,1)} %param.27, bf16[4,768,512]{2,1,0:T(8,128)(2,1)} %get-tuple-element.734, bf16[4,768,512]{2,1,0:T(8,128)(2,1)S(1)} %get-tuple-element.733), kind=kOutput, calls=%fused_computation.121 | convolution fusion | flops 6458179584 | bytes 20971520 | tf_op jit(solution)/shard_map/ecf,edf->ecd/dot_general | solution.py:261
  335.7 7.1 bitcast_convert_fusion
  342.9 7.3 bitcast_convert_fusion.1
  354.3 6.1 all-to-all-done
  360.4 31.8 %reduce-scatter.12.cloned.1.call-done = bf16[256,1024]{1,0:T(8,128)(2,1)} async-done(((bf16[2048,1024]{1,0:T(8,128)(2,1)}), bf16[256,1024]{1,0:T(8,128)(2,1)}) %reduce-scatter.12.cloned.1.call-update) | async-done | bytes 524304 | tf_op jit(solution)/shard_map/reduce_scatter | solution.py:270
  395.7 47.5 %reduce-scatter.10.cloned.1.call-done = bf16[256,1024]{1,0:T(8,128)(2,1)} async-done(((bf16[2048,1024]{1,0:T(8,128)(2,1)}), bf16[256,1024]{1,0:T(8,128)(2,1)}) %reduce-scatter.10.cloned.1.call-update) | async-done | bytes 524304 | tf_op jit(solution)/shard_map/reduce_scatter | solution.py:237
  450.0 27.8 %while.52 = (s32[]{:T(128)}, f32[8,2,256]{2,1,0:T(2,128)S(1)}, s32[4,512]{1,0:T(4,128)S(1)}, s32[4,512]{1,0:T(4,128)S(1)}, s32[256]{0:T(256)S(1)}, /*index=5*/bf...) while((s32[]{:T(128)}, f32[8,2,256]{2,1,0:T(2,128)S(1)}, ...), condition=%wide.region_29.30_spmd.clone, body=%wide.region_27.29_spmd.clone.sunk | while | flops 549982976 | bytes 21333164 | solution.py:300
  477.8 78.5 %while.53 = (s32[]{:T(128)}, f32[256,8,2,64]{0,3,2,1:T(8,128)S(1)}, bf16[4,512,8,64]{1,3,2,0:T(8,128)(2,1)}, bf16[4,512,8,64]{1,3,2,0:T(8,128)(2,1)}, bf16[4,512...) while((s32[]{:T(128)}, f32[256,8,2,64]{0,3,2,1:T(8,128)S(1)}, ...), condition=%wide.region_31.32_spmd.clone, body=%wide.region_30.31_spmd.clone.sunk | while | flops 1368916736 | bytes 132057888 | solution.py:332
  480.5 4.6 fusion.237
  500.1 4.6 fusion.237
  519.8 4.6 fusion.237
  539.4 4.6 fusion.237
  569.6 25.9 %reduce-scatter.14.cloned.1.call-done = bf16[256,512]{0,1:T(8,128)(2,1)} async-done(((bf16[2048,512]{0,1:T(8,128)(2,1)}), bf16[256,512]{0,1:T(8,128)(2,1)}) %reduce-scatter.14.cloned.1.call-update) | async-done | bytes 262160 | tf_op jit(solution)/shard_map/reduce_scatter | solution.py:336
  596.6 36.2 %reduce-scatter.16.cloned.1.call-done = bf16[256,512]{0,1:T(8,128)(2,1)} async-done(((bf16[2048,512]{0,1:T(8,128)(2,1)}), bf16[256,512]{0,1:T(8,128)(2,1)}) %reduce-scatter.16.cloned.1.call-update) | async-done | bytes 262160 | tf_op jit(solution)/shard_map/reduce_scatter | solution.py:339
  637.4 13.0 %convolution_convert_fusion = bf16[4,1024,1024]{2,1,0:T(8,128)(2,1)} fusion(bf16[4,768,1024]{2,1,0:T(8,128)(2,1)} %bitcast.374, bf16[4,768,512]{2,1,0:T(8,128)(2,1)} %get-tuple-element.734, bf16[4,768,512]{2,1,0:T(8,128)(2,1)} %copy-done.60), kind=kOutput, calls=%fused_computation.106 | convolution fusion | flops 6459228160 | bytes 20971520 | tf_op jit(solution)/shard_map/ecd,ecf->edf/dot_general | solution.py:260
  652.0 7.9 convolution_convert_fusion.2
  659.9 9.6 reduce-scatter.20.cloned.1.call-done
  669.5 51.2 %reduce-scatter.18.cloned.1.call-done = bf16[128,2048]{1,0:T(8,128)(2,1)} async-done(((bf16[1024,2048]{1,0:T(8,128)(2,1)}), bf16[128,2048]{1,0:T(8,128)(2,1)}) %reduce-scatter.18.cloned.1.call-update) | async-done | bytes 524304 | tf_op jit(solution)/shard_map/reduce_scatter | solution.py:363
  722.6 29.5 %reduce-scatter.22.cloned.1.call-done = bf16[128,32]{1,0:T(8,128)(2,1)} async-done(((bf16[1024,32]{1,0:T(8,128)(2,1)}), bf16[128,32]{1,0:T(8,128)(2,1)}) %reduce-scatter.22.cloned.1.call-update) | async-done | bytes 8208
  756.8 13.8 %all-reduce.2 = (bf16[1024]{0:T(1024)(128)(2,1)S(1)}, bf16[1024]{0:T(1024)(128)(2,1)S(1)}) all-reduce(bf16[1024]{0:T(1024)(128)(2,1)S(1)} %get-tuple-element.616, bf16[1024]{0:T(1024)(128)(2,1)S(1)} %copy-done.54), channel_id=6, replica_groups=mesh['rep'=4,'shard'=8] {'shard'}, use_global_device_ids=true, to_apply=%region_36.37.clone | all-reduce | flops 2048 | bytes 8192
  770.8 11.0 %all-reduce.3 = (bf16[128]{0:T(256)(128)(2,1)S(1)}, bf16[128]{0:T(256)(128)(2,1)S(1)}, bf16[128,32]{0,1:T(8,128)(2,1)S(1)}) all-reduce(bf16[128]{0:T(256)(128)(2,1)S(1)} %dynamic-slice.1, bf16[128]{0:T(256)(128)(2,1)S(1)} %dynamic-slice.3, bf16[128,32]{0,1:T(8,128)(2,1)S(1)} %copy.192), channel_id=1, replica_groups=mesh['rep'=4,'shard'=8] {'rep'}, use_global_device_ids=true, to_apply=%region_37.38 | all-reduce | flops 4352 | bytes 17408 | tf_op jit(solution)/shard_map/psum | solution.py:377
  784.7 225.6 %all-reduce.7.cloned.1.call-done = (bf16[128,2048]{1,0:T(8,128)(2,1)}, bf16[128,1024]{1,0:T(8,128)(2,1)}, bf16[4,1024,1024]{2,1,0:T(8,128)(2,1)}, bf16[4,512,1024]{2,1,0:T(8,128)(2,1)}) async-done(((bf16[128,2048]{1,0:T(8,128)(2,1)}, bf16[128,1024]{1,0:T(8,128)(2,1)}, bf16[4,1024,1024]{2,1,0:T(8,128)(2,1)}, bf16[4,512,1024]{2,1,0:T(8,128)(2,1)}), (bf16[128,2048]{1,0:T(8,128)(2,1)}, ...) | async-done | bytes 13369360 | tf_op jit(solution)/shard_map/psum | solution.py:378
  1010.4 11.9 %convert_element_type.238 = f32[4,1024,1024]{2,1,0:T(8,128)} convert(bf16[4,1024,1024]{2,1,0:T(8,128)(2,1)} %get-tuple-element.719) | non-fusion elementwise | flops 4194304 | bytes 25165824 | tf_op jit(solution)/shard_map/convert_element_type | solution.py:382
  (387 shorter events, 197.0 us)
Async XLA Ops:
  7.2 52.3 %all-gather.9.cloned.1.call-start = ((), (), s32[]{:S(2)}) async-start(), calls=%async_computation.8 | async-start | bytes 4718592 | tf_op jit(solution)/shard_map/all_gather | solution.py:84
  7.9 86.3 %all-gather.13.cloned.1.call-start = ((), (), s32[]{:S(2)}) async-start(), calls=%async_computation.10 | async-start | bytes 2359296 | tf_op jit(solution)/shard_map/all_gather | solution.py:116
  21.5 44.0 %copy-start.48 = (f32[8,1,128]{2,1,0:T(1,128)}, f32[8,1,128]{2,1,0:T(1,128)S(1)}, u32[]{:S(2)}) copy-start(f32[8,1,128]{2,1,0:T(1,128)S(1)} %convert_element_type.241) | copy-start | bytes 12292
  23.6 42.7 %copy-start.58 = (bf16[128]{0:T(256)(128)(2,1)S(1)}, bf16[128]{0:T(256)(128)(2,1)}, u32[]{:S(2)}) copy-start(bf16[128]{0:T(256)(128)(2,1)} %param.25) | copy-start | bytes 772
  23.6 53.5 %copy-start.55 = (f32[256]{0:T(256)}, f32[256]{0:T(256)S(1)}, u32[]{:S(2)}) copy-start(f32[256]{0:T(256)S(1)} %add_rsqrt_fusion.1) | copy-start | bytes 3076
  64.5 70.8 %all-gather.11.cloned.1.call-start = ((), (), s32[]{:S(2)}) async-start(), calls=%async_computation.9 | async-start | bytes 2359296 | tf_op jit(solution)/shard_map/all_gather | solution.py:117
  65.5 97.9 %all-gather.15.cloned.1.call-start = ((), (), s32[]{:S(2)}) async-start(), calls=%async_computation.11 | async-start | bytes 2359296 | tf_op jit(solution)/shard_map/all_gather | solution.py:85
  66.1 149.1 %all-gather.17.cloned.1.call-start = ((), (), s32[]{:S(2)}) async-start(), calls=%async_computation.12 | async-start | bytes 4718592 | tf_op jit(solution)/shard_map/all_gather | solution.py:180
  161.4 57.5 %copy-start.3 = (bf16[4,512,8,64]{1,3,2,0:T(8,128)(2,1)}, bf16[4,512,8,64]{1,3,2,0:T(8,128)(2,1)S(1)}, u32[]{:S(2)}) copy-start(bf16[4,512,8,64]{1,3,2,0:T(8,128)(2,1)S(1)} %get-tuple-element.1232) | copy-start | bytes 6291460
  163.4 55.5 %copy-start.16 = (bf16[256,8,2,64]{0,3,2,1:T(8,128)(2,1)}, bf16[256,8,2,64]{0,3,2,1:T(8,128)(2,1)S(1)}, u32[]{:S(2)}) copy-start(bf16[256,8,2,64]{0,3,2,1:T(8,128)(2,1)S(1)} %convert_element_type.199) | copy-start | bytes 1572868
  168.1 94.4 %all-gather.19.cloned.1.call-start = ((), (), s32[]{:S(2)}) async-start(), calls=%async_computation.14 | async-start | bytes 4718592 | tf_op jit(solution)/shard_map/all_gather | solution.py:181
  168.7 223.6 %reduce-scatter.12.cloned.1.call-start = ((), (), s32[]{:S(2)}) async-start(), calls=%async_computation.15 | async-start | bytes 4718592 | tf_op jit(solution)/shard_map/reduce_scatter | solution.py:270
  296.0 14.1 %copy-start.12 = (bf16[4,512,1024]{2,1,0:T(8,128)(2,1)S(1)}, bf16[4,512,1024]{2,1,0:T(8,128)(2,1)}, u32[]{:S(2)}) copy-start(bf16[4,512,1024]{2,1,0:T(8,128)(2,1)} %param.28) | copy-start | bytes 12582916
  322.1 13.6 %copy-start.60 = (bf16[4,768,512]{2,1,0:T(8,128)(2,1)}, bf16[4,768,512]{2,1,0:T(8,128)(2,1)S(1)}, u32[]{:S(2)}) copy-start(bf16[4,768,512]{2,1,0:T(8,128)(2,1)S(1)} %get-tuple-element.733) | copy-start | bytes 9437188
  342.8 100.4 %reduce-scatter.10.cloned.1.call-start = ((), (), s32[]{:S(2)}) async-start(), calls=%async_computation.13 | async-start | bytes 4718592 | tf_op jit(solution)/shard_map/reduce_scatter | solution.py:237
  342.9 49.3 %copy-start.10 = (f32[256,1024]{1,0:T(8,128)S(1)}, f32[256,1024]{1,0:T(8,128)}, u32[]{:S(2)}) copy-start(f32[256,1024]{1,0:T(8,128)} %copy-done.9) | copy-start | bytes 3145732
  342.9 49.3 %copy-start.47 = (f32[256]{0:T(256)S(1)}, f32[256]{0:T(256)}, u32[]{:S(2)}) copy-start(f32[256]{0:T(256)} %copy-done.46) | copy-start | bytes 3076
  350.3 99.6 %copy-start.31 = (pred[256,32]{0,1:T(8,128)(4,1)}, pred[256,32]{0,1:T(8,128)(4,1)S(1)}, u32[]{:S(2)}) copy-start(pred[256,32]{0,1:T(8,128)(4,1)S(1)} %fusion.121) | copy-start | bytes 24580
  350.6 99.3 %copy-start.22 = (f32[256,32]{0,1:T(8,128)}, f32[256,32]{0,1:T(8,128)S(1)}, u32[]{:S(2)}) copy-start(f32[256,32]{0,1:T(8,128)S(1)} %get-tuple-element.760) | copy-start | bytes 98308
  350.6 99.3 %copy-start.40 = (f32[256]{0:T(256)}, f32[256]{0:T(256)S(1)}, u32[]{:S(2)}) copy-start(f32[256]{0:T(256)S(1)} %get-tuple-element.759) | copy-start | bytes 3076
  350.7 99.3 %copy-start.34 = (s32[4,512]{1,0:T(4,128)S(1)}, s32[4,512]{1,0:T(4,128)}, u32[]{:S(2)}) copy-start(s32[4,512]{1,0:T(4,128)} %copy-done.33) | copy-start | bytes 24580
  350.7 99.3 %copy-start.45 = (f32[8,2,256]{2,1,0:T(2,128)S(1)}, f32[8,2,256]{2,1,0:T(2,128)}, u32[]{:S(2)}) copy-start(f32[8,2,256]{2,1,0:T(2,128)} %copy-done.44) | copy-start | bytes 49156
  350.7 9.7 all-to-all-start
  354.2 241.4 %reduce-scatter.14.cloned.1.call-start = ((), (), s32[]{:S(2)}) async-start(), calls=%async_computation.16 | async-start | bytes 2359296 | tf_op jit(solution)/shard_map/reduce_scatter | solution.py:336
  354.2 95.7 %copy-start.42 = (f32[256]{0:T(256)}, f32[256]{0:T(256)S(1)}, u32[]{:S(2)}) copy-start(f32[256]{0:T(256)S(1)} %fusion.128) | copy-start | bytes 3076
  360.3 89.6 %copy-start.24 = (f32[256,32]{0,1:T(8,128)}, f32[256,32]{0,1:T(8,128)S(1)}, u32[]{:S(2)}) copy-start(f32[256,32]{0,1:T(8,128)S(1)} %all_to_all.14) | copy-start | bytes 98308
  360.4 89.6 %copy-start.51 = (f32[256]{0:T(256)}, f32[256]{0:T(256)S(1)}, u32[]{:S(2)}) copy-start(f32[256]{0:T(256)S(1)} %multiply_reduce_fusion.5) | copy-start | bytes 3076
  446.2 121.0 %copy-start.7 = (f32[256,1024]{1,0:T(8,128)}, f32[256,1024]{1,0:T(8,128)S(1)}, u32[]{:S(2)}) copy-start(f32[256,1024]{1,0:T(8,128)S(1)} %get-tuple-element.739) | copy-start | bytes 3145732
  561.5 71.3 %reduce-scatter.16.cloned.1.call-start = ((), (), s32[]{:S(2)}) async-start(), calls=%async_computation.17 | async-start | bytes 2359296 | tf_op jit(solution)/shard_map/reduce_scatter | solution.py:339
  567.1 65.7 %copy-start.18 = (bf16[256,1024]{1,0:T(8,128)(2,1)S(1)}, bf16[256,1024]{1,0:T(8,128)(2,1)}, u32[]{:S(2)}) copy-start(bf16[256,1024]{1,0:T(8,128)(2,1)} %param.19) | copy-start | bytes 1572868
  567.1 65.7 %copy-start.49 = (f32[8,1,128]{2,1,0:T(1,128)S(1)}, f32[8,1,128]{2,1,0:T(1,128)}, u32[]{:S(2)}) copy-start(f32[8,1,128]{2,1,0:T(1,128)} %copy-done.48) | copy-start | bytes 12292
  567.1 65.7 %copy-start.56 = (f32[256]{0:T(256)S(1)}, f32[256]{0:T(256)}, u32[]{:S(2)}) copy-start(f32[256]{0:T(256)} %copy-done.55) | copy-start | bytes 3076
  567.2 102.3 %reduce-scatter.20.cloned.1.call-start = ((), (), s32[]{:S(2)}) async-start(), calls=%async_computation.19 | async-start | bytes 2359296 | tf_op jit(solution)/shard_map/reduce_scatter | solution.py:366
  569.3 151.4 %reduce-scatter.18.cloned.1.call-start = ((), (), s32[]{:S(2)}) async-start(), calls=%async_computation.18 | async-start | bytes 4718592 | tf_op jit(solution)/shard_map/reduce_scatter | solution.py:363
  569.6 67.7 %copy-start.29 = (bf16[256,16,64]{0,2,1:T(8,128)(2,1)}, bf16[256,16,64]{0,2,1:T(8,128)(2,1)S(1)}, u32[]{:S(2)}) copy-start(bf16[256,16,64]{0,2,1:T(8,128)(2,1)S(1)} %pad_maximum_fusion.7) | copy-start | bytes 1572868
  637.3 13.2 %copy-start.23 = (f32[256,32]{0,1:T(8,128)S(1)}, f32[256,32]{0,1:T(8,128)}, u32[]{:S(2)}) copy-start(f32[256,32]{0,1:T(8,128)} %copy-done.22) | copy-start | bytes 98308
  637.3 13.2 %copy-start.25 = (f32[256,32]{0,1:T(8,128)S(1)}, f32[256,32]{0,1:T(8,128)}, u32[]{:S(2)}) copy-start(f32[256,32]{0,1:T(8,128)} %copy-done.24) | copy-start | bytes 98308
  637.3 13.2 %copy-start.32 = (pred[256,32]{0,1:T(8,128)(4,1)S(1)}, pred[256,32]{0,1:T(8,128)(4,1)}, u32[]{:S(2)}) copy-start(pred[256,32]{0,1:T(8,128)(4,1)} %copy-done.31) | copy-start | bytes 24580
  637.3 13.2 %copy-start.41 = (f32[256]{0:T(256)S(1)}, f32[256]{0:T(256)}, u32[]{:S(2)}) copy-start(f32[256]{0:T(256)} %copy-done.40) | copy-start | bytes 3076
  637.4 14.6 %copy-start.6 = (bf16[4,768,512]{2,1,0:T(8,128)(2,1)S(1)}, bf16[4,768,512]{2,1,0:T(8,128)(2,1)}, u32[]{:S(2)}) copy-start(bf16[4,768,512]{2,1,0:T(8,128)(2,1)} %multiply_convert_fusion.3) | copy-start | bytes 9437188
  637.4 114.8 %reduce-scatter.22.cloned.1.call-start = ((), (), s32[]{:S(2)}) async-start(), calls=%async_computation.20 | async-start | bytes 294912
  651.8 358.6 %all-reduce.7.cloned.1.call-start = ((), (), s32[]{:S(2)}) async-start(), calls=%async_computation.21 | async-start | bytes 26738688 | tf_op jit(solution)/shard_map/psum | solution.py:378
  720.8 32.2 %copy-start.19 = (bf16[256,1024]{1,0:T(8,128)(2,1)S(1)}, bf16[256,1024]{1,0:T(8,128)(2,1)}, u32[]{:S(2)}) copy-start(bf16[256,1024]{1,0:T(8,128)(2,1)} %param.19) | copy-start | bytes 1572868
  720.8 32.2 %copy-start.30 = (bf16[256,16,64]{0,2,1:T(8,128)(2,1)S(1)}, bf16[256,16,64]{0,2,1:T(8,128)(2,1)}, u32[]{:S(2)}) copy-start(bf16[256,16,64]{0,2,1:T(8,128)(2,1)} %copy-done.29) | copy-start | bytes 1572868
  720.8 32.2 %copy-start.50 = (f32[8,1,128]{2,1,0:T(1,128)S(1)}, f32[8,1,128]{2,1,0:T(1,128)}, u32[]{:S(2)}) copy-start(f32[8,1,128]{2,1,0:T(1,128)} %copy-done.48) | copy-start | bytes 12292
  720.8 32.2 %copy-start.57 = (f32[256]{0:T(256)S(1)}, f32[256]{0:T(256)}, u32[]{:S(2)}) copy-start(f32[256]{0:T(256)} %copy-done.55) | copy-start | bytes 3076
  720.8 36.0 %copy-start.54 = (bf16[1024]{0:T(1024)(128)(2,1)S(1)}, bf16[1024]{0:T(1024)(128)(2,1)}, u32[]{:S(2)}) copy-start(bf16[1024]{0:T(1024)(128)(2,1)} %get-tuple-element.614) | copy-start | bytes 6148
  720.8 62.7 %copy-start.8 = (f32[256,1024]{1,0:T(8,128)S(1)}, f32[256,1024]{1,0:T(8,128)}, u32[]{:S(2)}) copy-start(f32[256,1024]{1,0:T(8,128)} %copy-done.7) | copy-start | bytes 3145732
  (43 other events, 209.8 us)
Sparse Core Ops, SparseCore 0:
  9.6 49.8 all-gather.8
  64.7 29.5 all-gather.12
  96.4 29.8 all-gather.10
  127.8 28.1 all-gather.14
  168.2 46.9 all-gather.16
  216.6 45.8 all-gather.18
  342.9 49.2 reduce-scatter.11
  395.1 48.1 reduce-scatter.9
  561.6 33.8 reduce-scatter.13
  598.3 34.5 reduce-scatter.15
  635.1 34.3 reduce-scatter.19
  672.2 48.4 reduce-scatter.17
  723.6 28.5 reduce-scatter.21
  757.1 253.2 all-reduce.6

commit v2 on v0

v2 whole, which is shorter than its diff:
```python
import functools

import jax
import jax.numpy as jnp
from jax import lax
from jax.experimental import pallas as pl
from jax.experimental.pallas import tpu as pltpu
from jax.sharding import PartitionSpec as P

HEADS = 16
KV_HEADS = 8
HEAD = 64
EXPERTS = 32
FF = 512
TOPK = 8
CAP = 96
EPSILON = 1e-06


NEG = -1e30
KEYS = 512
LANES = 128


def swap_halves(x):
    lane = lax.broadcasted_iota(jnp.int32, x.shape, 1)
    return jnp.where(lane % HEAD < HEAD // 2, pltpu.roll(x, LANES - HEAD // 2, 1), pltpu.roll(x, HEAD // 2, 1))


def nt_dot(a, b):
    return lax.dot_general(a, b, (((1,), (1,)), ((), ())), preferred_element_type=jnp.float32)


def nn_dot(a, b):
    return jnp.dot(a, b, preferred_element_type=jnp.float32)


def split_kv(kv, low_lane):
    turned = pltpu.roll(kv, HEAD, 1)
    keys = (jnp.where(low_lane, kv, 0.0), jnp.where(low_lane, 0.0, turned))
    vals = (jnp.where(low_lane, turned, 0.0), jnp.where(low_lane, 0.0, kv))
    return keys, vals


def allowed_mask(lo, hi, query_base, start_row):
    key = lo + lax.broadcasted_iota(jnp.int32, (hi - lo, start_row.shape[1]), 0)
    query = query_base + lax.broadcasted_iota(jnp.int32, (hi - lo, start_row.shape[1]), 1)
    return (key <= query) & (key >= start_row)


def causal_chunks(block, prompt_blocks, span):
    free = min(block, prompt_blocks) * span
    end = (block + 1) * span
    cuts = [(k, min(k + KEYS, free), False) for k in range(0, free, KEYS)]
    return cuts + [(k, min(k + KEYS, end), True) for k in range(free, end, KEYS)]


def attend_forward_kernel(
    x_ref, gain_ref, w_ref, cos_ref, sin_ref, wout_ref, start_ref,
    part_ref, first_ref, q_ref, kv_ref, mix_ref, lse_ref,
    keys_s, vals_s, qt_s, s_s, p_s, acc_s,
):
    block = pl.program_id(0)
    span = q_ref.shape[0]
    blocks = keys_s.shape[1] // span
    x = x_ref[...].astype(jnp.float32)
    inv = lax.rsqrt(jnp.mean(x * x, axis=1, keepdims=True) + EPSILON)
    first = (x * inv * gain_ref[...]).astype(jnp.bfloat16)
    first_ref[...] = first
    qkv = nn_dot(first, w_ref[...])
    lane = lax.broadcasted_iota(jnp.int32, (span, LANES), 1)
    low_lane = lane < HEAD
    cosine, sine = cos_ref[...], sin_ref[...]
    q = qkv[:, :LANES]
    q = q * cosine + swap_halves(q) * sine
    kv = qkv[:, LANES:]
    kv = jnp.where(low_lane, kv * cosine + swap_halves(kv) * sine, kv)
    q_ref[...] = q.astype(jnp.bfloat16)
    kv_ref[...] = kv.astype(jnp.bfloat16)
    keys, unused = split_kv(kv, low_lane)
    here = pl.ds(pl.multiple_of(block * span, span), span)
    for h in range(2):
        keys_s[h, here] = keys[h].astype(jnp.bfloat16)
    vals_s[:, here] = jnp.transpose(kv)[HEAD:].astype(jnp.bfloat16)
    qt_s[...] = (jnp.transpose(q.astype(jnp.bfloat16).astype(jnp.float32)) * HEAD**-0.5).astype(jnp.bfloat16)

    def attend(i):
        chunks = causal_chunks(i, blocks // 2, span)
        end = (i + 1) * span
        q_t = qt_s[...]
        start_row = start_ref[...]
        for h in range(2):
            top = jnp.full((1, span), NEG, jnp.float32)
            for lo, hi, masked in chunks:
                s = nn_dot(keys_s[h, lo:hi], q_t)
                if masked:
                    s = jnp.where(allowed_mask(lo, hi, i * span, start_row), s, NEG)
                s_s[h, lo:hi] = s
                top = jnp.maximum(top, jnp.max(s, axis=0, keepdims=True))
            total = jnp.zeros((1, span), jnp.float32)
            for lo, hi, masked in chunks:
                p = jnp.exp(s_s[h, lo:hi] - top)
                total = total + jnp.sum(p, axis=0, keepdims=True)
                p_s[h, lo:hi] = p.astype(jnp.bfloat16)
            acc_s[h * HEAD : (h + 1) * HEAD] = nn_dot(vals_s[:, :end], p_s[h, :end]) / total
            lse_ref[h : h + 1, :] = top + jnp.log(total)

    for i in range(blocks):
        pl.when(block == i)(functools.partial(attend, i))
    mix_t = acc_s[...]
    mix_ref[...] = mix_t.astype(jnp.bfloat16)
    part_ref[...] = nn_dot(jnp.transpose(mix_t).astype(jnp.bfloat16), wout_ref[...]).astype(jnp.bfloat16)


def attend_backward_kernel(
    shards, da_ref, q_ref, kv_ref, mix_ref, lse_ref, start_ref, wout_ref, w_ref, first_ref, cos_ref, sin_ref,
    oparts_ref, residual_ref, dfirst_ref, gw_ref, gout_ref, out_ref,
    keys_s, vals_s, keyt_s, dk_s, dv_s, dq_s, dqt_s, gw_s, gout_s, p_s, ds_s, *scratch
):
    block = pl.program_id(0)
    span = q_ref.shape[0]
    blocks = keys_s.shape[1] // span
    fwd = Collect(shards // 2, oparts_ref, scratch)

    @pl.when(block == 0)
    def _():
        greet_shard(shards)
        fwd.start()

    lane = lax.broadcasted_iota(jnp.int32, (span, LANES), 1)
    low_lane = lane < HEAD

    @pl.when(block == 0)
    def _():
        def prepare(j, c):
            here = pl.ds(pl.multiple_of(j * span, span), span)
            kv = kv_ref[here].astype(jnp.float32)
            keys, vals = split_kv(kv, low_lane)
            for h in range(2):
                keys_s[h, here] = keys[h].astype(jnp.bfloat16)
                vals_s[h, here] = vals[h].astype(jnp.bfloat16)
            keyt_s[:, here] = jnp.transpose(kv)[:HEAD].astype(jnp.bfloat16)
            dk_s[here] = jnp.zeros((span, LANES), jnp.float32)
            dv_s[here] = jnp.zeros((span, LANES), jnp.float32)
            return c

        lax.fori_loop(0, blocks, prepare, 0)
        gout_s[...] = jnp.zeros_like(gout_s)
        gw_s[...] = jnp.zeros_like(gw_s)

    da = da_ref[...]
    dm_f = nt_dot(da, wout_ref[...])
    dm = dm_f.astype(jnp.bfloat16)
    dm_tf = jnp.transpose(dm.astype(jnp.float32))
    dm_t = dm_tf.astype(jnp.bfloat16)
    gout_s[...] += nn_dot(mix_ref[...], da)
    prod = mix_ref[...].astype(jnp.float32) * dm_tf
    delta = [jnp.sum(prod[h * HEAD : (h + 1) * HEAD], axis=0, keepdims=True) for h in range(2)]
    qs_f = q_ref[...].astype(jnp.float32) * HEAD**-0.5
    qs = qs_f.astype(jnp.bfloat16)
    q_t = jnp.transpose(qs_f).astype(jnp.bfloat16)

    def attend(i):
        chunks = causal_chunks(i, blocks // 2, span)
        end = (i + 1) * span
        start_row = start_ref[...]
        for h in range(2):
            for lo, hi, masked in chunks:
                s = nn_dot(keys_s[h, lo:hi], q_t)
                if masked:
                    s = jnp.where(allowed_mask(lo, hi, i * span, start_row), s, NEG)
                p = jnp.exp(s - lse_ref[h : h + 1, :])
                dp = nn_dot(vals_s[h, lo:hi], dm_t)
                p_s[h, lo:hi] = p.astype(jnp.bfloat16)
                ds_s[h, lo:hi] = (p * (dp - delta[h])).astype(jnp.bfloat16)
            dqt_s[h * HEAD : (h + 1) * HEAD] = nn_dot(keyt_s[:, :end], ds_s[h, :end])
        for lo, hi, masked in chunks:
            low_key = lax.broadcasted_iota(jnp.int32, (hi - lo, LANES), 1) < HEAD
            dv_s[lo:hi] += jnp.where(low_key, nn_dot(p_s[0, lo:hi], dm), nn_dot(p_s[1, lo:hi], dm))
            dk_s[lo:hi] += jnp.where(low_key, nn_dot(ds_s[0, lo:hi], qs), nn_dot(ds_s[1, lo:hi], qs))

    for i in range(blocks):
        pl.when(block == i)(functools.partial(attend, i))
    dq_s[block] = jnp.transpose(dqt_s[...]) * HEAD**-0.5
    hops = list(range(shards // 2 - 1, 0, -1))
    turns = {}
    for k, hop in enumerate(hops):
        turns.setdefault(0 if k == 0 else blocks - len(hops) + k, []).append(hop)
    for turn_block, some in turns.items():
        pl.when(block == turn_block)(functools.partial(fwd.carry, some))

    @pl.when(block == blocks - 1)
    def _():
        def finish(j, c):
            here = pl.ds(pl.multiple_of(j * span, span), span)
            dk = dk_s[here]
            dk = dk + pltpu.roll(dk, HEAD, 1)
            dv = dv_s[here]
            dv = dv + pltpu.roll(dv, HEAD, 1)
            cosine, sine = cos_ref[j], sin_ref[j]
            dkv = jnp.where(low_lane, dk * cosine - swap_halves(dk) * sine, dv).astype(jnp.bfloat16)
            dq = dq_s[j]
            dq = (dq * cosine - swap_halves(dq) * sine).astype(jnp.bfloat16)
            d_qkv = jnp.concatenate([dq, dkv], axis=1)
            d_qkv_t = jnp.transpose(d_qkv.astype(jnp.float32)).astype(jnp.bfloat16)
            gw_s[...] += nn_dot(d_qkv_t, first_ref[j])
            dfirst_ref[j] = nt_dot(d_qkv, w_ref[...]).astype(jnp.bfloat16)
            return c

        lax.fori_loop(0, blocks, finish, 0)
        shards, lines = gw_ref.shape[:2]
        cols = gw_s.shape[1] // shards
        for k in range(shards):
            for p in range(LANES // cols):
                gw_ref[k, :, p * cols : (p + 1) * cols] = gw_s[
                    p * lines : (p + 1) * lines, k * cols : (k + 1) * cols
                ].astype(jnp.bfloat16)
        for k in range(gout_s.shape[1] // LANES):
            gout_ref[k * LANES : (k + 1) * LANES] = gout_s[:, k * LANES : (k + 1) * LANES].astype(jnp.bfloat16)

        def finish_out(here, total):
            out_ref[here] = (residual_ref[here] + total).astype(jnp.bfloat16)

        for cut in range(2):
            fwd.finish(cut, finish_out)
        fwd.settle()


def attend_forward(x, gain, w, cosine, sine, w_out, start):
    total, width = x.shape
    span = 512 if total <= 2048 else 256
    blocks = total // span
    row = lambda cols: pl.BlockSpec((span, cols), lambda i: (i, 0))
    col = lambda rows: pl.BlockSpec((rows, span), lambda i: (0, i))
    fixed = lambda shape: pl.BlockSpec(shape, lambda i: tuple(0 for s in shape), pipeline_mode=pl.Buffered(1))
    shape = jax.ShapeDtypeStruct
    return pl.pallas_call(
        attend_forward_kernel,
        grid_spec=pltpu.PrefetchScalarGridSpec(
            num_scalar_prefetch=0,
            grid=(blocks,),
            in_specs=[row(width), fixed((1, width)), fixed(w.shape), row(LANES), row(LANES), fixed(w_out.shape), col(1)],
            out_specs=[row(width), row(width), row(LANES), row(LANES), col(LANES), col(2)],
            scratch_shapes=[
                pltpu.VMEM((2, total, LANES), jnp.bfloat16),
                pltpu.VMEM((HEAD, total), jnp.bfloat16),
                pltpu.VMEM((LANES, span), jnp.bfloat16),
                pltpu.VMEM((2, total, span), jnp.float32),
                pltpu.VMEM((2, total, span), jnp.bfloat16),
                pltpu.VMEM((LANES, span), jnp.float32),
            ],
        ),
        out_shape=[
            shape((total, width), jnp.bfloat16),
            shape((total, width), jnp.bfloat16),
            shape((total, LANES), jnp.bfloat16),
            shape((total, LANES), jnp.bfloat16),
            shape((LANES, total), jnp.bfloat16),
            shape((2, total), jnp.float32),
        ],
        compiler_params=pltpu.CompilerParams(dimension_semantics=("arbitrary",), vmem_limit_bytes=60 << 20),
        cost_estimate=cost(17),
        name="attend_forward",
    )(x, gain, w, cosine, sine, w_out, start)


def attend_backward(d_attn, q, kv, mix, lse, start, w_out, w, first, cosine, sine, o_parts, residual, shards):
    total, width = d_attn.shape
    span = 512 if total <= 2048 else 256
    blocks = total // span
    cols = w.shape[1]
    row = lambda cols: pl.BlockSpec((span, cols), lambda i: (i, 0))
    col = lambda rows: pl.BlockSpec((rows, span), lambda i: (0, i))
    fixed = lambda shape: pl.BlockSpec(shape, lambda i: tuple(0 for s in shape), pipeline_mode=pl.Buffered(1))
    shape = jax.ShapeDtypeStruct
    cut = lambda a: a.reshape(blocks, span, a.shape[1])
    return pl.pallas_call(
        functools.partial(attend_backward_kernel, shards),
        grid_spec=pltpu.PrefetchScalarGridSpec(
            num_scalar_prefetch=0,
            grid=(blocks,),
            in_specs=[
                row(width), row(LANES), fixed((total, LANES)), col(LANES), col(2), col(1),
                fixed(w_out.shape), fixed(w.shape), fixed((blocks, span, width)),
                fixed((blocks, span, LANES)), fixed((blocks, span, LANES)), ANY, fixed(residual.shape),
            ],
            out_specs=[fixed((blocks, span, width)), fixed((shards, cols * width // shards // LANES, LANES)), fixed((width, LANES)), fixed(residual.shape)],
            scratch_shapes=[
                pltpu.VMEM((2, total, LANES), jnp.bfloat16),
                pltpu.VMEM((2, total, LANES), jnp.bfloat16),
                pltpu.VMEM((HEAD, total), jnp.bfloat16),
                pltpu.VMEM((total, LANES), jnp.float32),
                pltpu.VMEM((total, LANES), jnp.float32),
                pltpu.VMEM((blocks, span, LANES), jnp.float32),
                pltpu.VMEM((LANES, span), jnp.float32),
                pltpu.VMEM((cols, width), jnp.float32),
                pltpu.VMEM(w_out.shape, jnp.float32),
                pltpu.VMEM((2, total, span), jnp.bfloat16),
                pltpu.VMEM((2, total, span), jnp.bfloat16),
            ]
            + Collect.boxes(shards, *residual.shape),
        ),
        out_shape=[
            shape((blocks, span, width), jnp.bfloat16),
            shape((shards, cols * width // shards // LANES, LANES), jnp.bfloat16),
            shape((width, LANES), jnp.bfloat16),
            shape(residual.shape, jnp.bfloat16),
        ],
        compiler_params=remote_params(5, 60),
        cost_estimate=cost(34),
        name="attend_backward",
    )(d_attn, q, kv, mix, lse, start, w_out, w, cut(first), cut(cosine), cut(sine), o_parts, residual)


MESH = pl.DeviceIdType.MESH


def chip_spot():
    me = lax.axis_index("shard")
    return me, me // 2, me % 2


def greet(others):
    barrier = pltpu.get_barrier_semaphore()
    for other in others:
        pl.semaphore_signal(barrier, inc=1, device_id=other, device_id_type=MESH)
    pl.semaphore_wait(barrier, len(others))


def greet_shard(shards):
    me = lax.axis_index("shard")
    greet([{"shard": lax.rem(me + k, shards)} for k in range(1, shards)])


def remote(src, dst, send_sem, recv_sem, target):
    return pltpu.make_async_remote_copy(
        src_ref=src,
        dst_ref=dst,
        send_sem=send_sem,
        recv_sem=recv_sem,
        device_id=target,
        device_id_type=MESH,
    )


def halves(rows):
    first = rows // 32 * 16
    return [(0, first), (first, rows - first)]


class Spread:
    def __init__(self, chips, src, out, sems):
        self.chips, self.src, self.out = chips, src, out
        self.own_sem, self.right_sem, self.left_sem, self.cross_sem, self.recv_sem = sems
        self.me, self.chip, self.core = chip_spot()
        self.cuts = halves(out.shape[1])
        self.has_right, self.has_left = self.chip < chips - 1, self.chip > 0

    @staticmethod
    def sems(shards):
        dma = pltpu.SemaphoreType.DMA
        return [dma((2,)), dma((shards,)), dma((shards,)), dma((shards,)), dma((2 * shards,))]

    def copy(self, way, source, cut, from_src=False, core=None):
        block = 2 * source + (self.core if core is None else core)
        here = pl.ds(*self.cuts[cut])
        sem = dict(right=self.right_sem, left=self.left_sem, cross=self.cross_sem)[way].at[2 * source + cut]
        target = dict(right=self.me + 2, left=self.me - 2, cross=2 * self.chip + 1 - self.core)[way]
        held = self.src.at[here] if from_src else self.out.at[block, here]
        return remote(held, self.out.at[block, here], sem, self.recv_sem.at[2 * block + cut], {"shard": target})

    def own(self, cut):
        here = pl.ds(*self.cuts[cut])
        return pltpu.make_async_copy(self.src.at[here], self.out.at[self.me, here], self.own_sem.at[cut])

    def start(self, cut):
        pl.when(self.has_right)(lambda: self.copy("right", self.chip, cut, True).start())
        pl.when(self.has_left)(lambda: self.copy("left", self.chip, cut, True).start())
        self.copy("cross", self.chip, cut, True).start()
        self.own(cut).start()

    def each(self, action, tick=lambda: None):
        for hop in range(1, self.chips):
            for cut in range(2):
                for side in (-1, 1):
                    source = self.chip + side * hop
                    inside = (source >= 0) if side < 0 else (source < self.chips)
                    pl.when(inside)(functools.partial(action, source, side, cut))
                    tick()

    def carry(self, tick=lambda: None):
        def pass_on(source, side, cut):
            self.copy("cross", source, cut).wait_recv()
            if side < 0:
                pl.when(self.has_right)(lambda: self.copy("right", source, cut).start())
            else:
                pl.when(self.has_left)(lambda: self.copy("left", source, cut).start())
            self.copy("cross", source, cut).start()

        self.each(pass_on, tick)

    def settle(self):
        for source in range(self.chips):
            for cut in range(2):
                self.copy("cross", source, cut, core=1 - self.core).wait_recv()
        for cut in range(2):
            self.own(cut).wait()
            self.copy("cross", self.chip, cut, True).wait_send()
            pl.when(self.has_right)(lambda cut=cut: self.copy("right", self.chip, cut, True).wait_send())
            pl.when(self.has_left)(lambda cut=cut: self.copy("left", self.chip, cut, True).wait_send())

        def sent(source, side, cut):
            if side < 0:
                pl.when(self.has_right)(lambda: self.copy("right", source, cut).wait_send())
            else:
                pl.when(self.has_left)(lambda: self.copy("left", source, cut).wait_send())
            self.copy("cross", source, cut).wait_send()

        self.each(sent)


STRIP = 16


class Collect:
    def __init__(self, chips, parts, boxes):
        self.chips, self.parts = chips, parts
        self.mine, self.cross, self.inbox = boxes[:3]
        self.mine_sem, self.swap_send, self.swap_recv, self.on_send, self.right_recv, self.left_recv = boxes[3:]
        self.me, self.chip, self.core = chip_spot()
        self.cuts = halves(parts.shape[1])

    @staticmethod
    def boxes(shards, rows, width):
        chips = shards // 2
        box = lambda count: pltpu.VMEM((count, rows, width), jnp.bfloat16)
        dma = pltpu.SemaphoreType.DMA
        return [box(chips), box(chips), box(chips + 1), dma((chips,))] + [dma((shards,))] * 5

    def load(self, dest):
        return pltpu.make_async_copy(self.parts.at[2 * dest + self.core], self.mine.at[dest], self.mine_sem.at[dest])

    def swap(self, dest, cut):
        here, sem = pl.ds(*self.cuts[cut]), 2 * dest + cut
        return remote(
            self.parts.at[2 * dest + 1 - self.core, here], self.cross.at[dest, here],
            self.swap_send.at[sem], self.swap_recv.at[sem], {"shard": 2 * self.chip + 1 - self.core},
        )

    def slot(self, dest, side, chip):
        return dest if side > 0 else jnp.where(dest == chip, self.chips, dest)

    def onward(self, dest, side, cut):
        here, at = pl.ds(*self.cuts[cut]), 2 * dest + cut
        slot = self.slot(dest, side, self.chip + side)
        sem, target = (self.right_recv, self.me + 2) if side > 0 else (self.left_recv, self.me - 2)
        return remote(
            self.cross.at[dest, here], self.inbox.at[slot, here], self.on_send.at[at], sem.at[at], {"shard": target}
        )

    def arrived(self, dest, side, cut):
        here, at = pl.ds(*self.cuts[cut]), 2 * dest + cut
        box = self.inbox.at[self.slot(dest, side, self.chip)]
        sem = self.right_recv if side > 0 else self.left_recv
        remote(box.at[here], box.at[here], self.on_send.at[at], sem.at[at], {"shard": 2 * self.chip + 1 - self.core}).wait_recv()
        return box

    def each(self, action, hops=None, tick=lambda: None):
        for hop in range(self.chips - 1, 0, -1) if hops is None else hops:
            for cut in range(2):
                for side in (1, -1):
                    dest = self.chip + side * hop
                    inside = (dest < self.chips) if side > 0 else (dest >= 0)
                    pl.when(inside)(functools.partial(action, dest, side, cut))
                    tick()

    def start(self):
        def begin(dest, side, cut):
            self.swap(dest, cut).start()
            if cut == 0:
                self.load(dest).start()

        self.each(begin)
        for cut in range(2):
            self.swap(self.chip, cut).start()
        self.load(self.chip).start()

    def strips(self, cut, parts, store):
        base, size = self.cuts[cut]

        def body(i, c):
            here = pl.ds(pl.multiple_of(base + i * STRIP, STRIP), STRIP)
            total = parts[0][here].astype(jnp.float32)
            for part in parts[1:]:
                total = total + part[here].astype(jnp.float32)
            store(here, total)
            return c

        lax.fori_loop(0, size // STRIP, body, 0)

    def carry(self, hops=None, tick=lambda: None):
        def pass_on(dest, side, cut):
            if cut == 0:
                self.load(dest).wait()
            self.swap(dest, cut).wait_recv()
            inner = (self.chip > 0) if side > 0 else (self.chip < self.chips - 1)
            near = (self.mine.at[dest], self.cross.at[dest])

            def keep(here, total):
                self.cross[dest, here] = total.astype(jnp.bfloat16)

            pl.when(inner)(lambda: self.strips(cut, near + (self.arrived(dest, side, cut),), keep))
            pl.when(jnp.logical_not(inner))(lambda: self.strips(cut, near, keep))
            self.onward(dest, side, cut).start()

        self.each(pass_on, hops, tick)

    def finish(self, cut, store):
        chip = self.chip
        if cut == 0:
            self.load(chip).wait()
        self.swap(chip, cut).wait_recv()
        near = (self.mine.at[chip], self.cross.at[chip])

        @pl.when((chip > 0) & (chip < self.chips - 1))
        def _():
            both = (self.arrived(chip, 1, cut), self.arrived(chip, -1, cut))
            self.strips(cut, near + both, store)

        pl.when(chip == 0)(lambda: self.strips(cut, near + (self.arrived(chip, -1, cut),), store))
        pl.when(chip == self.chips - 1)(lambda: self.strips(cut, near + (self.arrived(chip, 1, cut),), store))

    def settle(self):
        for cut in range(2):
            self.swap(self.chip, cut).wait_send()
        self.each(lambda dest, side, cut: self.swap(dest, cut).wait_send())
        self.each(lambda dest, side, cut: self.onward(dest, side, cut).wait_send())


class Direct:
    def __init__(self, shards, src, out, send_sem, recv_sem):
        self.shards, self.src, self.out, self.send_sem, self.recv_sem = shards, src, out, send_sem, recv_sem
        self.me = lax.axis_index("shard")

    @staticmethod
    def sems(shards):
        return [pltpu.SemaphoreType.DMA((shards,)), pltpu.SemaphoreType.DMA((shards,))]

    def copy(self, k):
        target = lax.rem(self.me + k, self.shards)
        return remote(
            self.src(target), self.out(self.me), self.send_sem.at[k], self.recv_sem.at[self.me], {"shard": target}
        )

    def own(self):
        return pltpu.make_async_copy(self.src(self.me), self.out(self.me), self.send_sem.at[0])

    def start(self):
        self.own().start()
        for k in range(1, self.shards):
            self.copy(k).start()

    def settle(self):
        self.own().wait()
        for k in range(1, self.shards):
            source = lax.rem(self.me + k, self.shards)
            block = self.out(source)
            remote(block, block, self.send_sem.at[k], self.recv_sem.at[source], {"shard": source}).wait_recv()
        for k in range(1, self.shards):
            self.copy(k).wait_send()


ANY = pl.BlockSpec(memory_space=pl.ANY)
INNER = pl.BlockSpec(memory_space=pltpu.VMEM)


def remote_params(call, megabytes):
    return pltpu.CompilerParams(collective_id=call, has_side_effects=True, vmem_limit_bytes=megabytes << 20)


def cost(micros):
    return pl.CostEstimate(flops=0, bytes_accessed=int(micros * 3.2e6), transcendentals=0)


def open_kernel(shards, x_ref, small_ref, choice_ref, piece_ref, all_x, all_small, all_choice, all_piece, *sems):
    greet_shard(shards)
    spread = Spread(shards // 2, x_ref, all_x, sems[:5])
    for cut in range(2):
        spread.start(cut)
    direct = [
        Direct(shards, lambda target: piece_ref.at[target], lambda source: all_piece.at[source], *sems[5:7]),
        Direct(shards, lambda target: small_ref, lambda source: all_small.at[source], *sems[7:9]),
        Direct(shards, lambda target: choice_ref, lambda source: all_choice.at[source], *sems[9:11]),
    ]
    for one in direct:
        one.start()
    spread.carry()
    for one in direct:
        one.settle()
    spread.settle()


def open_gathers(x, small, choice, pieces, shards):
    wide = lambda a: jax.ShapeDtypeStruct((shards,) + a.shape, a.dtype)
    return pl.pallas_call(
        functools.partial(open_kernel, shards),
        out_shape=[wide(x), wide(small), wide(choice), jax.ShapeDtypeStruct(pieces.shape, pieces.dtype)],
        in_specs=[ANY] * 4,
        out_specs=[ANY] * 4,
        scratch_shapes=Spread.sems(shards) + Direct.sems(shards) * 3,
        compiler_params=remote_params(1, 60),
        cost_estimate=cost(45),
        name="open_gathers",
    )(x, small, choice, pieces)


def expert_ids(shape, per_row):
    row = lax.broadcasted_iota(jnp.int32, shape, 0)
    rows = EXPERTS // per_row
    return per_row * (row % rows) + row // rows


def gate_columns(logits, choice, ids):
    named = jnp.zeros(logits.shape, jnp.float32)
    for k in range(choice.shape[0]):
        named = jnp.where(choice[k : k + 1] == ids, 1.0, named)
    masked = jnp.where(named > 0, logits, NEG)
    weight = jnp.where(named > 0, jnp.exp(masked - jnp.max(masked, axis=0, keepdims=True)), 0.0)
    return weight / jnp.sum(weight, axis=0, keepdims=True)


def middle_kernel(
    shards, parts_ref, x_ref, gain_ref, router_ref, choice_ref, residual_ref, second_ref, gates_ref, all_ref, *scratch
):
    greet_shard(shards)
    chips = shards // 2
    collect = Collect(chips, parts_ref, scratch[:9])
    spread = Spread(chips, second_ref, all_ref, scratch[9:14])
    collect.start()
    collect.carry()
    for cut in range(2):

        def store(here, total):
            residual = x_ref[here].astype(jnp.float32) + total
            residual_ref[here] = residual
            inv = lax.rsqrt(jnp.mean(residual * residual, axis=1, keepdims=True) + EPSILON)
            second_ref[here] = (residual * inv * gain_ref[...]).astype(jnp.bfloat16)

        collect.finish(cut, store)
        spread.start(cut)
    logits = nt_dot(router_ref[...], second_ref[...])
    per_row = x_ref.shape[1] // x_ref.shape[0]
    gates_ref[...] = gate_columns(logits, choice_ref[...], expert_ids(logits.shape, per_row))
    spread.carry()
    collect.settle()
    spread.settle()


def middle(parts, x, gain, router_t, choice_t, shards):
    rows, width = x.shape
    shape = jax.ShapeDtypeStruct
    return pl.pallas_call(
        functools.partial(middle_kernel, shards),
        out_shape=[
            shape((rows, width), jnp.float32),
            shape((rows, width), jnp.bfloat16),
            shape((EXPERTS, rows), jnp.float32),
            shape((shards, rows, width), jnp.bfloat16),
        ],
        in_specs=[ANY] + [INNER] * 4,
        out_specs=[INNER] * 3 + [ANY],
        scratch_shapes=Collect.boxes(shards, rows, width) + Spread.sems(shards),
        compiler_params=remote_params(2, 60),
        cost_estimate=cost(75),
        name="middle",
    )(parts.reshape(shards, rows, width), x, gain, router_t, choice_t)


def turn_kernel(
    shards, reps, parts_ref, gd_ref, residual_ref, cot_ref, gain_ref, gates_ref, second_ref, router_ref,
    dres_ref, dgain_ref, drouter_ref, all_ref, gdsum_ref, dsec_s, datt_s, *scratch
):
    me = lax.axis_index("shard")
    greet([{"shard": lax.rem(me + k, shards)} for k in range(1, shards)] + Exchange.partners(reps))
    chips = shards // 2
    rows, width = residual_ref.shape
    collect = Collect(chips, parts_ref, scratch[:9])
    spread = Spread(chips, datt_s, all_ref, scratch[9:14])
    sums = GridSum(reps, [(gd_ref.at[e], gdsum_ref.at[e]) for e in range(gd_ref.shape[0])], scratch[14:23])
    collect.start()
    sums.begin()
    steps = sums.steps()
    tick = lambda: next(steps, None)
    collect.carry(tick=tick)

    def stash(here, total):
        dsec_s[here] = total

    for cut in range(2):
        collect.finish(cut, stash)
    lines = EXPERTS * rows // width
    d_gates = dsec_s[rows : rows + lines] + dsec_s[rows + lines : rows + 2 * lines]
    d_gates = jnp.concatenate([d_gates[:, k * rows : (k + 1) * rows] for k in range(width // rows)], axis=0)
    gates = gates_ref[...]
    d_logits = gates * (d_gates - jnp.sum(gates * d_gates, axis=0, keepdims=True))
    high = d_logits.astype(jnp.bfloat16)
    low = (d_logits - high.astype(jnp.float32)).astype(jnp.bfloat16)
    drouter_ref[...] = nn_dot(high, second_ref[...]) + nn_dot(low, second_ref[...])
    dgain_ref[...] = jnp.zeros_like(dgain_ref)
    high_t = jnp.transpose(high.astype(jnp.float32)).astype(jnp.bfloat16)
    low_t = jnp.transpose(low.astype(jnp.float32)).astype(jnp.bfloat16)
    for cut in range(2):
        half = rows // 2
        for k in range(2):
            here = slice(cut * half + k * half // 2, cut * half + (k + 1) * half // 2)
            d_second = dsec_s[here] + nn_dot(high_t[here], router_ref[...]) + nn_dot(low_t[here], router_ref[...])
            residual = residual_ref[here]
            inv = lax.rsqrt(jnp.mean(residual * residual, axis=1, keepdims=True) + EPSILON)
            normed = residual * inv
            dgain_ref[...] += jnp.sum(d_second * normed, axis=0, keepdims=True)
            d_norm = d_second * gain_ref[...]
            d_residual = cot_ref[here].astype(jnp.float32) + inv * (
                d_norm - normed * jnp.mean(d_norm * normed, axis=1, keepdims=True)
            )
            dres_ref[here] = d_residual
            datt_s[here] = d_residual.astype(jnp.bfloat16)
        spread.start(cut)
    spread.carry(tick)
    for unused in steps:
        pass
    collect.settle()
    spread.settle()


def turn(parts, grad_down, residual, cot, gain, gates, second, router_t, shards, reps):
    rows, width = residual.shape
    shape = jax.ShapeDtypeStruct
    return pl.pallas_call(
        functools.partial(turn_kernel, shards, reps),
        out_shape=[
            shape((rows, width), jnp.float32),
            shape((1, width), jnp.float32),
            shape((EXPERTS, width), jnp.float32),
            shape((shards, rows, width), jnp.bfloat16),
            shape(grad_down.shape, jnp.bfloat16),
        ],
        in_specs=[ANY] * 2 + [INNER] * 6,
        out_specs=[INNER] * 3 + [ANY] * 2,
        scratch_shapes=[
            pltpu.VMEM((parts.shape[1], width), jnp.float32),
            pltpu.VMEM((rows, width), jnp.bfloat16),
        ]
        + Collect.boxes(shards, parts.shape[1], width)
        + Spread.sems(shards)
        + GridSum.scratch(reps, grad_down.shape[0], grad_down.shape[1], width),
        compiler_params=remote_params(3, 60),
        cost_estimate=cost(75),
        name="turn",
    )(parts, grad_down, residual, cot, gain, gates, second, router_t)


class Exchange:
    def __init__(self, reps, data, boxes, send_sem, recv_sem):
        self.data, self.boxes, self.send_sem, self.recv_sem = data, boxes, send_sem, recv_sem
        self.rep = lax.axis_index("rep")
        self.bits = reps.bit_length() - 1
        half = data.shape[0] // 2
        self.cuts = [(0, half), (half, half)]

    @staticmethod
    def scratch(reps, rows, dtype):
        bits = reps.bit_length() - 1
        dma = pltpu.SemaphoreType.DMA((2 * bits,))
        return [pltpu.VMEM((bits, rows, LANES), dtype), dma, dma]

    @staticmethod
    def partners(reps):
        rep = lax.axis_index("rep")
        bits = [1 << k for k in range(reps.bit_length() - 1)]
        return [{"rep": rep + bit - 2 * bit * ((rep // bit) % 2)} for bit in bits]

    def copy(self, stage, cut):
        here, sem = pl.ds(*self.cuts[cut]), 2 * stage + cut
        bit = 1 << (stage if cut == 0 else self.bits - 1 - stage)
        other = self.rep + bit - 2 * bit * ((self.rep // bit) % 2)
        return remote(
            self.data.at[here], self.boxes.at[stage, here], self.send_sem.at[sem], self.recv_sem.at[sem], {"rep": other}
        )

    def run(self, store):
        for cut in range(2):
            self.copy(0, cut).start()
        for stage in range(self.bits):
            for cut in range(2):
                copy = self.copy(stage, cut)
                copy.wait_recv()
                copy.wait_send()
                base, size = self.cuts[cut]
                strip = 64 if size % 64 == 0 else size

                def body(i, c):
                    here = pl.ds(pl.multiple_of(base + i * strip, 8), strip)
                    total = self.data[here].astype(jnp.float32) + self.boxes[stage, here].astype(jnp.float32)
                    if stage == self.bits - 1:
                        store(here, total)
                    else:
                        self.data[here] = total.astype(self.data.dtype)
                    return c

                lax.fori_loop(0, size // strip, body, 0)
                if stage < self.bits - 1:
                    self.copy(stage + 1, cut).start()


class GridSum:
    def __init__(self, reps, pieces, scratch):
        self.pieces, self.bits = pieces, reps.bit_length() - 1
        self.full, self.inbox, self.result = scratch[:3]
        self.load_sem, self.store_sem, self.down_send, self.down_recv, self.up_send, self.up_recv = scratch[3:]
        self.rep = lax.axis_index("rep")
        self.rows = self.full.shape[1]

    @staticmethod
    def scratch(reps, count, rows, width):
        bits = reps.bit_length() - 1
        dma = pltpu.SemaphoreType.DMA
        return [
            pltpu.VMEM((count, rows, width), jnp.bfloat16),
            pltpu.VMEM((count, rows, width), jnp.bfloat16),
            pltpu.VMEM((count, rows, width), jnp.bfloat16),
            dma((count,)),
            dma((count,)),
        ] + [dma((count, bits))] * 4

    def spot(self, piece, stage):
        base, size = 0, self.rows
        bits = []
        for k in range(stage + 1):
            which = k if piece % 2 == 0 else self.bits - 1 - k
            bits.append((which, (self.rep // (1 << which)) % 2))
        for which, bit in bits[:-1]:
            size //= 2
            base = base + bit * size
        which, bit = bits[-1]
        size //= 2
        kept = pl.multiple_of(base + bit * size, size)
        given = pl.multiple_of(base + (1 - bit) * size, size)
        partner = self.rep + (1 << which) - 2 * (1 << which) * bit
        return kept, given, size, {"rep": partner}

    def box_at(self, stage):
        return sum(self.rows >> (k + 1) for k in range(stage))

    def down(self, piece, stage):
        kept, given, size, partner = self.spot(piece, stage)
        return remote(
            self.full.at[piece, pl.ds(given, size)], self.inbox.at[piece, pl.ds(self.box_at(stage), size)],
            self.down_send.at[piece, stage], self.down_recv.at[piece, stage], partner,
        )

    def up(self, piece, stage, given=False):
        kept, other, size, partner = self.spot(piece, stage)
        here = self.result.at[piece, pl.ds(other if given else kept, size)]
        return remote(here, here, self.up_send.at[piece, stage], self.up_recv.at[piece, stage], partner)

    def load(self, piece):
        return pltpu.make_async_copy(self.pieces[piece][0], self.full.at[piece], self.load_sem.at[piece])

    def store(self, piece):
        return pltpu.make_async_copy(self.result.at[piece], self.pieces[piece][1], self.store_sem.at[piece])

    def add(self, piece, stage):
        kept, given, size, partner = self.spot(piece, stage)
        strip = 32

        def body(i, c):
            here = pl.ds(pl.multiple_of(kept + i * strip, strip), strip)
            there = pl.ds(pl.multiple_of(self.box_at(stage) + i * strip, strip), strip)
            total = self.full[piece, here].astype(jnp.float32) + self.inbox[piece, there].astype(jnp.float32)
            held = self.result if stage == self.bits - 1 else self.full
            held[piece, here] = total.astype(jnp.bfloat16)
            return c

        lax.fori_loop(0, size // strip, body, 0)

    def begin(self):
        for piece in range(len(self.pieces)):
            self.load(piece).start()
        for piece in range(len(self.pieces)):
            self.load(piece).wait()
            self.down(piece, 0).start()

    def steps(self):
        count, bits = len(self.pieces), self.bits
        for stage in range(bits):
            for piece in range(count):
                self.down(piece, stage).wait_recv()
                self.add(piece, stage)
                (self.down(piece, stage + 1) if stage < bits - 1 else self.up(piece, stage)).start()
                yield
        for stage in range(bits - 1, -1, -1):
            for piece in range(count):
                self.up(piece, stage, True).wait_recv()
                (self.up(piece, stage - 1) if stage else self.store(piece)).start()
                yield
        for piece in range(count):
            for stage in range(bits):
                self.down(piece, stage).wait_send()
                self.up(piece, stage).wait_send()
            self.store(piece).wait()


MINI = 48


def close_kernel(
    shards, reps, dparts_ref, x_ref, dres_ref, gain_ref, head_ref, outg_ref, drouter_ref,
    dgain_ref, dtok_ref, share_ref, small_ref, bulk_s, mini_s, sum_s, minis_s, *scratch
):
    me = lax.axis_index("shard")
    greet([{"shard": lax.rem(me + k, shards)} for k in range(1, shards)] + Exchange.partners(reps))
    chips = shards // 2
    tok = Collect(chips, dparts_ref, scratch[:9])
    piece = head_ref.shape[1]
    bulk_at = lambda source: bulk_s.at[pl.ds(pl.multiple_of(source * piece, piece), piece)]
    heads = Direct(shards, lambda target: head_ref.at[target], bulk_at, *scratch[9:11])
    mini = Direct(shards, lambda target: mini_s.at[target], lambda source: minis_s.at[source], *scratch[11:13])
    bulk_sum = Exchange(reps, bulk_s, *scratch[13:16])
    mini_sum = Exchange(reps, sum_s, *scratch[16:19])
    tok.start()
    heads.start()
    bulk_s[shards * piece :] = outg_ref[...]
    cols = gain_ref.shape[1] // shards
    mini_s[...] = jnp.zeros_like(mini_s)
    for k in range(shards):
        here = slice(k * cols, (k + 1) * cols)
        mini_s[k, :EXPERTS, :cols] = drouter_ref[:, here]
        mini_s[k, EXPERTS : EXPERTS + 1, :cols] = dgain_ref[:, here]
    tok.carry()

    def finish_tok(here, d_first):
        x = x_ref[here].astype(jnp.float32)
        inv = lax.rsqrt(jnp.mean(x * x, axis=1, keepdims=True) + EPSILON)
        normed = x * inv
        term = jnp.sum(d_first * normed, axis=0, keepdims=True)
        for k in range(shards):
            mini_s[k, EXPERTS + 1 : EXPERTS + 2, :cols] += term[:, k * cols : (k + 1) * cols]
        d_norm = d_first * gain_ref[...]
        dtok_ref[here] = dres_ref[here] + inv * (d_norm - normed * jnp.mean(d_norm * normed, axis=1, keepdims=True))

    for cut in range(2):
        tok.finish(cut, finish_tok)
    mini.start()
    heads.settle()

    def keep_bulk(here, total):
        share_ref[here] = total

    bulk_sum.run(keep_bulk)
    mini.settle()
    total = minis_s[0]
    for k in range(1, shards):
        total = total + minis_s[k]
    sum_s[...] = total

    def keep_mini(here, total):
        small_ref[here] = total

    mini_sum.run(keep_mini)
    tok.settle()


def close(d_parts, x, d_residual, gain, head_parts, out_grad, d_router, d_gain, shards, reps):
    rows, width = x.shape
    shape = jax.ShapeDtypeStruct
    piece = head_parts.shape[1]
    bulk = shards * piece + out_grad.shape[0]
    f32, bf16 = jnp.float32, jnp.bfloat16
    deep = lambda a: a.reshape(shards, rows, width)
    return pl.pallas_call(
        functools.partial(close_kernel, shards, reps),
        out_shape=[
            shape((rows, width), f32),
            shape((bulk, LANES), f32),
            shape((MINI, LANES), f32),
        ],
        in_specs=[ANY] + [INNER] * 7,
        out_specs=[INNER] * 3,
        scratch_shapes=[
            pltpu.VMEM((bulk, LANES), bf16),
            pltpu.VMEM((shards, MINI, LANES), f32),
            pltpu.VMEM((MINI, LANES), f32),
            pltpu.VMEM((shards, MINI, LANES), f32),
        ]
        + Collect.boxes(shards, rows, width)
        + Direct.sems(shards) * 2
        + Exchange.scratch(reps, bulk, bf16)
        + Exchange.scratch(reps, MINI, f32),
        compiler_params=remote_params(4, 60),
        cost_estimate=cost(70),
        name="close",
    )(deep(d_parts), x, d_residual, gain, head_parts, out_grad, d_router, d_gain)


def tn_dot(a, b):
    return lax.dot_general(a, b, (((0,), (0,)), ((), ())), preferred_element_type=jnp.float32)


def slot_picks(choice, first_expert, local):
    rows = choice.shape[1]
    named = []
    for e in range(8):
        hit = jnp.zeros((1, rows), jnp.float32)
        if e < local:
            hit = jnp.max(jnp.where(choice == first_expert + e, 1.0, 0.0), axis=0, keepdims=True)
        named.append(hit)
    named = jnp.concatenate(named, axis=0)
    earlier = lax.broadcasted_iota(jnp.int32, (rows, rows), 0) < lax.broadcasted_iota(jnp.int32, (rows, rows), 1)
    rank = nn_dot(named.astype(jnp.bfloat16), jnp.where(earlier, 1.0, 0.0).astype(jnp.bfloat16))
    rank = jnp.where(named > 0, rank, -1.0)
    slot = lax.broadcasted_iota(jnp.int32, (CAP, rows), 0).astype(jnp.float32)
    return [jnp.where(rank[e : e + 1] == slot, 1.0, 0.0) for e in range(local)]


def pick_kernel(first_ref, x_ref, g_ref, choice_ref, router_ref, xs_ref, gs_ref, gate_ref):
    local = xs_ref.shape[0]
    rows = x_ref.shape[1]
    x, choice, first_expert = x_ref[0], choice_ref[0], first_ref[0]
    logits = nt_dot(router_ref[...], x)
    ids = expert_ids(logits.shape, x.shape[1] // x.shape[0])
    gates = gate_columns(logits, choice, ids)
    picks = slot_picks(choice, first_expert, local)
    for e in range(local):
        own = jnp.sum(jnp.where(ids == first_expert + e, gates, 0.0), axis=0, keepdims=True)
        gate_ref[e, 0] = jnp.sum(picks[e] * own, axis=1, keepdims=True)
    pick = jnp.concatenate(picks, axis=0).astype(jnp.bfloat16)
    xs = nn_dot(pick, x).astype(jnp.bfloat16)
    gs = nn_dot(pick, g_ref[0]).astype(jnp.bfloat16)
    for e in range(local):
        xs_ref[e, 0] = xs[e * CAP : (e + 1) * CAP]
        gs_ref[e, 0] = gs[e * CAP : (e + 1) * CAP]


def expert_kernel(xs_ref, gs_ref, gate_ref, wgu_ref, wd_ref, y_ref, dy_ref, dgate_ref, ggu_ref, gd_ref, hid_s, dg_s, dgu_s):
    slots = xs_ref.shape[1]
    chunk = 256

    def part(i, c):
        here = pl.ds(pl.multiple_of(i * chunk, chunk), chunk)
        gate = gate_ref[0, here]
        gate_up = nn_dot(xs_ref[0, here], wgu_ref[0])
        gate_part, up_part = gate_up[:, :FF], gate_up[:, FF:]
        sig = 1.0 / (1.0 + jnp.exp(-gate_part))
        silu = gate_part * sig
        hidden = (silu * up_part).astype(jnp.bfloat16)
        hid_s[here] = hidden
        out = nn_dot(hidden, wd_ref[0])
        g = gs_ref[0, here].astype(jnp.float32)
        dgate_ref[0, here] = jnp.sum(out * g, axis=1, keepdims=True)
        y_ref[0, here] = (out * gate).astype(jnp.bfloat16)
        d_out = (g * gate).astype(jnp.bfloat16)
        dg_s[here] = d_out
        d_hidden = nt_dot(d_out, wd_ref[0])
        d_up = (d_hidden * silu).astype(jnp.bfloat16)
        d_gate = (d_hidden * up_part * (sig * (1.0 + gate_part * (1.0 - sig)))).astype(jnp.bfloat16)
        dgu = jnp.concatenate([d_gate, d_up], axis=1)
        dgu_s[here] = dgu
        dy_ref[0, here] = nt_dot(dgu, wgu_ref[0]).astype(jnp.bfloat16)
        return c

    lax.fori_loop(0, slots // chunk, part, 0)
    cols = 256
    for k in range(hid_s.shape[1] // cols):
        here = slice(k * cols, (k + 1) * cols)
        gd_ref[0, here, :] = tn_dot(hid_s[:, here], dg_s[...]).astype(jnp.bfloat16)
    for k in range(xs_ref.shape[2] // cols):
        here = slice(k * cols, (k + 1) * cols)
        ggu_ref[0, here, :] = tn_dot(xs_ref[0, :, here], dgu_s[...]).astype(jnp.bfloat16)


def combine_kernel(first_ref, choice_ref, y_ref, dy_ref, dgate_ref, out_ref, dout_ref):
    local = y_ref.shape[0]
    rows, width = out_ref.shape[1:]
    first_expert = first_ref[0]
    picks = slot_picks(choice_ref[0], first_expert, local)
    per_row = width // rows
    lines = EXPERTS // per_row
    line = lax.broadcasted_iota(jnp.int32, (lines, rows), 0)
    spots = [jnp.zeros((lines, rows), jnp.float32)] * per_row
    for e in range(local):
        d_gate = jnp.sum(picks[e] * dgate_ref[e, 0], axis=0, keepdims=True)
        for k in range(per_row):
            spots[k] = jnp.where(line * per_row + k == first_expert + e, d_gate, spots[k])
    d_gates = jnp.concatenate(spots, axis=1)
    high = d_gates.astype(jnp.bfloat16)
    low = (d_gates - high.astype(jnp.float32)).astype(jnp.bfloat16)
    dout_ref[0, rows:] = jnp.concatenate([high.astype(jnp.float32), low.astype(jnp.float32)], axis=0).astype(jnp.bfloat16)
    pick = jnp.concatenate(picks, axis=0).astype(jnp.bfloat16)
    out_ref[0] = tn_dot(pick, y_ref[:, 0].reshape(local * CAP, -1)).astype(jnp.bfloat16)
    dout_ref[0, :rows] = tn_dot(pick, dy_ref[:, 0].reshape(local * CAP, -1)).astype(jnp.bfloat16)


def run_experts(group_in, group_cot, group_choice, router_t, w_gate_up, w_down, first_expert):
    shards, rows, width = group_in.shape
    local = w_down.shape[0]
    slots = shards * CAP
    shape = jax.ShapeDtypeStruct
    params = lambda mb: pltpu.CompilerParams(dimension_semantics=("arbitrary",), vmem_limit_bytes=mb << 20)
    source = pl.BlockSpec((1, rows, width), lambda n, first: (n, 0, 0))
    named = pl.BlockSpec((1, TOPK, rows), lambda n, first: (n, 0, 0))
    placed = pl.BlockSpec((local, 1, CAP, width), lambda n, first: (0, n, 0, 0))
    thin = pl.BlockSpec((local, 1, CAP, 1), lambda n, first: (0, n, 0, 0))
    bf16, f32 = jnp.bfloat16, jnp.float32
    xs, gs, gates = pl.pallas_call(
        pick_kernel,
        grid_spec=pltpu.PrefetchScalarGridSpec(
            num_scalar_prefetch=1,
            grid=(shards,),
            in_specs=[source, source, named, pl.BlockSpec(router_t.shape, lambda n, first: (0, 0))],
            out_specs=[placed, placed, thin],
        ),
        out_shape=[
            shape((local, shards, CAP, width), bf16),
            shape((local, shards, CAP, width), bf16),
            shape((local, shards, CAP, 1), f32),
        ],
        compiler_params=params(60),
        cost_estimate=cost(8),
        name="pick_rows",
    )(first_expert, group_in, group_cot, group_choice, router_t)
    flat = lambda a: a.reshape(local, slots, a.shape[3])
    each = lambda r, c: pl.BlockSpec((1, r, c), lambda e: (e, 0, 0))
    y, dy, dgate, ggu, gd = pl.pallas_call(
        expert_kernel,
        grid=(local,),
        in_specs=[each(slots, width), each(slots, width), each(slots, 1), each(width, 2 * FF), each(FF, width)],
        out_specs=[each(slots, width), each(slots, width), each(slots, 1), each(width, 2 * FF), each(FF, width)],
        out_shape=[
            shape((local, slots, width), bf16),
            shape((local, slots, width), bf16),
            shape((local, slots, 1), f32),
            shape(w_gate_up.shape, bf16),
            shape(w_down.shape, bf16),
        ],
        scratch_shapes=[
            pltpu.VMEM((slots, FF), bf16),
            pltpu.VMEM((slots, width), bf16),
            pltpu.VMEM((slots, 2 * FF), bf16),
        ],
        compiler_params=params(60),
        cost_estimate=cost(42),
        name="experts",
    )(flat(xs), flat(gs), flat(gates), w_gate_up, w_down)
    deep = lambda a: a.reshape(local, shards, CAP, a.shape[2])
    extra = 2 * EXPERTS * rows // width
    out, d_out = pl.pallas_call(
        combine_kernel,
        grid_spec=pltpu.PrefetchScalarGridSpec(
            num_scalar_prefetch=1,
            grid=(shards,),
            in_specs=[named, placed, placed, thin],
            out_specs=[source, pl.BlockSpec((1, rows + extra, width), lambda n, first: (n, 0, 0))],
        ),
        out_shape=[
            shape((shards, rows, width), bf16),
            shape((shards, rows + extra, width), bf16),
        ],
        compiler_params=params(60),
        cost_estimate=cost(9),
        name="combine_rows",
    )(first_expert, group_choice, deep(y), deep(dy), deep(dgate))
    return out, d_out, ggu, gd


def layout(lengths, tok_index, prompt_len):
    order = jnp.arange(lengths.shape[0])
    starts = prompt_len + jnp.sum(jnp.where(order[None, :] < order[:, None], lengths[None, :], 0), axis=1)
    passed = tok_index[:, None] >= starts[None, :]
    seg_start = jnp.max(jnp.where(passed, starts[None, :], 0), axis=1)
    position = jnp.where(seg_start > 0, tok_index - seg_start + prompt_len, tok_index)
    return (seg_start, position)


def head_pieces(w_qkv, shards):
    rows = w_qkv.shape[0]
    query_width, key_width = HEADS * HEAD, KV_HEADS * HEAD
    part = w_qkv[:, :query_width].reshape(rows, shards, query_width // shards)
    part = jnp.pad(part, ((0, 0), (0, 0), (0, LANES - part.shape[2])))
    share = shards // KV_HEADS
    keys = jnp.repeat(
        w_qkv[:, query_width : query_width + key_width].reshape(rows, KV_HEADS, HEAD), share, axis=1
    )
    vals = jnp.repeat(w_qkv[:, query_width + key_width :].reshape(rows, KV_HEADS, HEAD), share, axis=1)
    return jnp.concatenate([part, keys, vals], axis=2).transpose(1, 0, 2)


def joined_heads(pieces, shards):
    rows = pieces.shape[2]
    query_part = HEADS * HEAD // shards
    share = shards // KV_HEADS
    query = pieces[:, :query_part].reshape(HEADS * HEAD, rows)
    key = jnp.sum(pieces[:, LANES : LANES + HEAD].reshape(KV_HEADS, share, HEAD, rows), axis=1)
    val = jnp.sum(pieces[:, LANES + HEAD :].reshape(KV_HEADS, share, HEAD, rows), axis=1)
    joined = jnp.concatenate(
        [query, key.reshape(KV_HEADS * HEAD, rows), val.reshape(KV_HEADS * HEAD, rows)], axis=0
    )
    return joined.T


def on_device(
    tokens, choices, cont_lengths, norm_attn, w_qkv, w_out, norm_ffn, w_router, w_gate_up, w_down, cotangent
):
    row_count, model_width = tokens.shape
    shards, reps = lax.axis_size("shard"), lax.axis_size("rep")
    group_len = row_count * shards
    prompt_len = group_len // 2
    own_rows = norm_attn.shape[0]
    per_row = model_width // row_count
    router_part = w_router.T.reshape(EXPERTS // per_row, per_row, own_rows).transpose(1, 0, 2)
    small = jnp.concatenate(
        [router_part.reshape(EXPERTS, own_rows), norm_attn[None], norm_ffn[None], jnp.zeros((6, own_rows), jnp.bfloat16)],
        axis=0,
    )
    choice_t = choices.T
    group_tokens, group_small, group_choice, w_heads = open_gathers(
        tokens, small, choice_t, head_pieces(w_qkv, shards), shards
    )
    held_cot, group_tokens = lax.optimization_barrier((cotangent, group_tokens))
    group_cot = lax.all_gather(held_cot, "shard", axis=0, tiled=True)
    group_small = group_small.transpose(1, 0, 2).reshape(small.shape[0], model_width)
    router_t = group_small[:EXPERTS]
    gain_attn = group_small[EXPERTS : EXPERTS + 1].astype(jnp.float32)
    gain_ffn = group_small[EXPERTS + 1 : EXPERTS + 2].astype(jnp.float32)
    w_heads = w_heads.reshape(model_width, 2 * LANES)
    own_out = jnp.pad(w_out, ((0, LANES - w_out.shape[0]), (0, 0)))
    group_index = jnp.arange(group_len, dtype=jnp.int32)
    seg_start, position = layout(cont_lengths[0], group_index, prompt_len)
    lane = jnp.arange(LANES, dtype=jnp.int32)
    half = HEAD // 2
    freq_table = 10000.0 ** (-(lane % half).astype(jnp.float32) / half)
    angle = position.astype(jnp.float32)[:, None] * freq_table[None, :]
    cosine = jnp.cos(angle)
    sine = jnp.sin(angle) * jnp.where(lane % HEAD < half, -1.0, 1.0)[None, :]
    start_row = seg_start[None, :]
    cosine, sine, start_row = lax.optimization_barrier((cosine, sine, start_row))
    out_parts, group_first, queries, key_values, mixed_t, log_total = attend_forward(
        group_tokens.reshape(group_len, model_width), gain_attn, w_heads, cosine, sine, own_out, start_row
    )
    residual, second_in, gates, group_in = middle(out_parts, tokens, gain_ffn, router_t, choice_t, shards)
    out_terms, d_terms, grad_gate_up, grad_down = run_experts(
        group_in, group_cot.reshape(group_in.shape), group_choice, router_t, w_gate_up, w_down,
        lax.axis_index("shard")[None] * w_down.shape[0],
    )
    grad_gate_up = lax.psum(grad_gate_up, "rep")
    d_residual, d_gain, d_router, group_d_attn, grad_down = turn(
        d_terms, grad_down, residual, cotangent, gain_ffn, gates, second_in, router_t, shards, reps
    )
    d_parts, head_parts, out_grad, output = attend_backward(
        group_d_attn.reshape(group_len, model_width), queries, key_values, mixed_t, log_total, start_row,
        own_out, w_heads, group_first, cosine, sine, out_terms, residual, shards,
    )
    d_tokens, share, small_sum = close(
        d_parts, tokens, d_residual, gain_attn, head_parts, out_grad, d_router, d_gain, shards, reps
    )
    lines = head_parts.shape[1]
    head_grads = share[: shards * lines].reshape(shards, lines, LANES // own_rows, own_rows)
    head_grads = head_grads.transpose(0, 2, 1, 3).reshape(shards, 2 * LANES, own_rows)
    out_share = share[shards * lines :].reshape(model_width // LANES, LANES, LANES).transpose(1, 0, 2)
    router_share = small_sum[:EXPERTS, :own_rows].reshape(per_row, EXPERTS // per_row, own_rows).transpose(2, 1, 0)
    return (
        output,
        d_tokens,
        small_sum[EXPERTS + 1, :own_rows],
        joined_heads(head_grads, shards),
        out_share.reshape(LANES, model_width)[: w_out.shape[0]],
        small_sum[EXPERTS, :own_rows],
        router_share.reshape(own_rows, EXPERTS),
        grad_gate_up.astype(jnp.float32),
        grad_down.astype(jnp.float32),
    )


def solution(mesh):
    return jax.shard_map(
        on_device,
        mesh=mesh,
        in_specs=(
            P(("rep", "shard"), None),
            P(("rep", "shard"), None),
            P("rep", None),
            P("shard"),
            P("shard", None),
            P("shard", None),
            P("shard"),
            P("shard", None),
            P("shard", None, None),
            P("shard", None, None),
            P(("rep", "shard"), None),
        ),
        out_specs=(
            P(("rep", "shard"), None),
            P(("rep", "shard"), None),
            P("shard"),
            P("shard", None),
            P("shard", None),
            P("shard"),
            P("shard", None),
            P("shard", None, None),
            P("shard", None, None),
        ),
        check_vma=False,
    )
```

time: 1480 us -> 573 us (0.39)
  waiting for transfers between devices: 756 us -> 0.06 us
  Pallas kernels: 0 us -> 509 us
  matrix products: 215 us -> 0 us
  blocking collectives: 193 us -> 0 us
  local copies, waits for them, and re-layouts: 198 us -> 12.5 us
  other arithmetic: 76.8 us -> 28.3 us
  starting transfers between devices: 20 us -> 0.08 us
    pallas_call x0 -> x9, Pallas kernels: none -> 509 us  [the longest x1 154 us: turn(): pl.pallas_call(functools.partial(turn_kernel, shards, reps), out_shape=[s...]
    all_to_all x4 -> x0, waiting for transfers between devices: 342 us -> none  [the longest x1 125 us: on_device(): lax.all_to_all(d_send, 'shard', split_axis=0, concat_axis=0, tiled=True)]
    psum x1, waiting for transfers between devices: 225 us -> 0.01 us  [on_device(): grad_gate_up = lax.psum(grad_gate_up, 'rep')]
    dot_general x51 -> x0, matrix products: 215 us -> none  [the longest x12 37.7 us: block_scores(): jnp.einsum('qgrd,kgd->grqk', queries, key_rot, preferred_element_type=jnp...]
    all_gather x3 -> x0, blocking collectives: 168 us -> none  [the longest x1 145 us: on_device(): lax.all_gather(w_router, 'shard', axis=0, tiled=True)]
    reduce_scatter x4 -> x0, waiting for transfers between devices: 123 us -> none  [the longest x1 51.7 us: on_device(): lax.psum_scatter(grad_qkv.astype(jnp.bfloat16), 'shard', scatter_dimensio...]
    gather x4 -> x0, local copies, waits for them, and re-layouts: 61.8 us -> none  [the longest x1 18.6 us: on_device(): d_padded[slot_pair].reshape(shard_count, CAP, local_experts, model_width)]
    reshape x10 -> x6, local copies, waits for them, and re-layouts: 60.4 us -> 2.18 us  [the longest x1 0.85 us: on_device(): out_share.reshape(LANES, model_width)[:w_out.shape[0]]]
  transfers between devices with their start and end apart: 14 -> 2, of which waited for: 10 -> 0; matrix products, arithmetic and copies ran while one was open for 17% -> 4% of each run, Pallas kernels for 0% -> 71%
where the time goes in v2:
time: 573 us; the launch traced here: 565 us
  Pallas kernels  509 us (89%)
  other arithmetic  28.3 us (5%)
  between operations  14.5 us (3%)
  local copies, waits for them, and re-layouts  12.5 us (2%)
    pallas_call x1, Pallas kernels, turn(): pl.pallas_call(functools.partial(turn_kernel, shards, reps), out_shape=[s...  154 us
    pallas_call x1, Pallas kernels, middle(): pl.pallas_call(functools.partial(middle_kernel, shards), out_shape=[shape...  86 us
    pallas_call x1, Pallas kernels, close(): pl.pallas_call(functools.partial(close_kernel, shards, reps), out_shape=[...  74.4 us
    pallas_call x1, Pallas kernels, attend_backward(): pl.pallas_call(functools.partial(attend_backward_kernel, shards), grid_sp...  55.4 us
    pallas_call x1, Pallas kernels, open_gathers(): pl.pallas_call(functools.partial(open_kernel, shards), out_shape=[wide(x)...  53.8 us
    pallas_call x1, Pallas kernels, run_experts(): pl.pallas_call(expert_kernel, grid=(local,), in_specs=[each(slots, width)...  41.6 us
    pallas_call x1, Pallas kernels, attend_forward(): pl.pallas_call(attend_forward_kernel, grid_spec=pltpu.PrefetchScalarGridS...  17.9 us
    pallas_call x1, Pallas kernels, run_experts(): pl.pallas_call(pick_kernel, grid_spec=pltpu.PrefetchScalarGridSpec(num_sc...  13 us
  transfers between devices with their start and end apart: 2, of which 0 were waited for; matrix products, arithmetic and copies ran while one was open for 4% of the time, Pallas kernels for 71%

profile of v2, /device:TPU:0, one launch (start us, length us, event | category | flops | bytes accessed | tf_op | source)
XLA Modules:
  0.0 564.6 jit_solution(16964184763186032561)
XLA Ops:
  7.2 0.0 copy-start.4
  7.2 0.0 all-gather.2.cloned.1.call-start
  7.3 1.0 slice.47
  8.2 1.0 fusion.10
  9.2 0.7 copy.62
  9.9 0.2 copy.53
  10.1 0.2 copy.44
  10.3 0.1 copy.54
  10.4 0.2 copy.45
  10.6 0.1 copy.55
  10.7 0.2 copy.46
  10.9 0.1 pad.9.clone
  11.0 1.0 maximum_bitcast_fusion.1.piece_ref
  12.0 0.0 copy-done.5
  12.0 0.7 maximum_maximum_fusion.small_ref
  12.7 53.8 %open_gathers.1 = (bf16[8,256,1024]{2,1,0:T(8,128)(2,1)}, bf16[8,40,128]{2,1,0:T(8,128)(2,1)}, s32[8,8,256]{2,1,0:T(8,128)}, bf16[8,128,256]{2,1,0:T(8,128)(2,1)}) custom-call(bf16[256,1024]{1,0:T(8,128)(2,1)} %x_ref.5, bf16[40,128]{1,0:T(8,128)(2,1)} %maximum_maximum_fusion.small_ref, s32[8,256]{1,0:T(8,128)} %bitcast.102, ...), custom_call_target="tpu_custom_call" | custom-call | bytes 144000000 | tf_op jit(solution)/shard_map/open_gathers/pallas_call | solution.py:605
  66.4 0.0 all-gather.2.cloned.1.call-update
  66.5 0.0 all-reduce.2.cloned.1.call-start
  66.5 0.1 fusion.4
  66.7 0.1 fusion.1
  66.8 5.6 fusion
  72.4 1.4 fusion.2
  73.8 17.9 %attend_forward.1 = (bf16[2048,1024]{1,0:T(8,128)(2,1)}, bf16[2048,1024]{1,0:T(8,128)(2,1)}, bf16[2048,128]{1,0:T(8,128)(2,1)}, bf16[2048,128]{1,0:T(8,128)(2,1)...) custom-call(bf16[2048,1024]{1,0:T(8,128)(2,1)} %bitcast.82, f32[1,1024]{1,0:T(1,128)} %get-tuple-element.96.gain_ref, ...), custom_call_target="tpu_custom_call" | custom-call | bytes 54400000 | tf_op jit(solution)/shard_map/attend_forward/pallas_call | solution.py:237
  91.7 0.6 copy_bitcast_fusion.1.router_ref
  92.3 86.0 %middle.1 = (f32[256,1024]{1,0:T(8,128)}, bf16[256,1024]{1,0:T(8,128)(2,1)}, f32[32,256]{1,0:T(8,128)}, bf16[8,256,1024]{2,1,0:T(8,128)(2,1)}) custom-call(bf16[8,256,1024]{2,1,0:T(8,128)(2,1)} %bitcast.83, bf16[256,1024]{1,0:T(8,128)(2,1)} %x_ref.5, f32[1,1024]{1,0:T(1,128)} %get-tuple-element.95.gain_ref, bf16[32,1024]{1,0:T(8,128)(2,1)} %copy_bitcast_fusion.1.router_ref, ...), custom_call_target="tpu_custom_call" | custom-call | bytes 240000000 | tf_op jit(solution)/shard_map/middle/pallas_call | solution.py:662
  178.3 0.0 all-gather.2.cloned.1.call-done
  178.3 13.0 %pick_rows.1 = (bf16[4,8,96,1024]{3,2,1,0:T(8,128)(2,1)}, bf16[4,8,96,1024]{3,2,1,0:T(8,128)(2,1)}, f32[4,8,96,1]{3,2,1,0:T(8,128)}) custom-call(s32[1]{0:T(128)} %bitcast.first_ref, bf16[8,256,1024]{2,1,0:T(8,128)(2,1)} %get-tuple-element.59.x_ref, bf16[8,256,1024]{2,1,0:T(8,128)(2,1)} %bitcast.81, s32[8,8,256]{2,1,0:T(8,128)} %get-tuple-element.50.choice_ref, ...), custom_call_target="tpu_custom_call" | custom-call | bytes 25600000 | tf_op jit(solution)/shard_map/pick_rows/pallas_call | solution.py:1114
  191.3 41.6 %experts.1 = (bf16[4,768,1024]{2,1,0:T(8,128)(2,1)}, bf16[4,768,1024]{2,1,0:T(8,128)(2,1)}, f32[4,768,1]{2,1,0:T(8,128)}, bf16[4,1024,1024]{2,1,0:T(8,128)(2,1)}, bf16[4,512,1024]{2,1,0:T(8,128)(2,1)}) custom-call(bf16[4,768,1024]{2,1,0:T(8,128)(2,1)} %bitcast.76, bf16[4,768,1024]{2,1,0:T(8,128)(2,1)} %bitcast.77, f32[4,768,1]{2,1,0:T(8,128)} %bitcast.90, ...), custom_call_target="tpu_custom_call" | custom-call | bytes 134400000 | tf_op jit(solution)/shard_map/experts/pallas_call | solution.py:1133
  232.9 0.0 all-reduce.2.cloned.1.call-update
  232.9 12.7 %combine_rows.1 = (bf16[8,256,1024]{2,1,0:T(8,128)(2,1)}, bf16[8,272,1024]{2,1,0:T(8,128)(2,1)}) custom-call(s32[1]{0:T(128)} %bitcast.first_ref, s32[8,8,256]{2,1,0:T(8,128)} %get-tuple-element.50.choice_ref, bf16[4,8,96,1024]{3,2,1,0:T(8,128)(2,1)} %bitcast.74, bf16[4,8,96,1024]{3,2,1,0:T(8,128)(2,1)} %bitcast.75, f32[4,8,96,1]{3,2,1,0:T(8,128)} %bitcast.91), custom_call_target="tpu_custom_call" | custom-call | bytes 28800000 | tf_op jit(solution)/shard_map/combine_rows/pallas_call | solution.py:1156
  245.6 154.4 %turn.1 = (f32[256,1024]{1,0:T(8,128)}, f32[1,1024]{1,0:T(1,128)}, f32[32,1024]{1,0:T(8,128)}, bf16[8,256,1024]{2,1,0:T(8,128)(2,1)}, bf16[4,512,1024]{2,1,0:T(8,128)(2,1)}) custom-call(bf16[8,272,1024]{2,1,0:T(8,128)(2,1)} %get-tuple-element.67.parts_ref, bf16[4,512,1024]{2,1,0:T(8,128)(2,1)} %get-tuple-element.68.gd_ref, ...), custom_call_target="tpu_custom_call" | custom-call | bytes 240000000 | tf_op jit(solution)/shard_map/turn/pallas_call | solution.py:738
  400.0 55.4 %attend_backward.1 = (bf16[4,512,1024]{2,1,0:T(8,128)(2,1)}, bf16[8,256,128]{2,1,0:T(8,128)(2,1)}, bf16[1024,128]{1,0:T(8,128)(2,1)}, bf16[256,1024]{1,0:T(8,128)(2,1)}) custom-call(bf16[2048,1024]{1,0:T(8,128)(2,1)} %bitcast.79, bf16[2048,128]{1,0:T(8,128)(2,1)} %get-tuple-element.73.q_ref, bf16[2048,128]{1,0:T(8,128)(2,1)} %get-tuple-element.74.kv_ref, ...), custom_call_target="tpu_custom_call" | custom-call | bytes 108800000 | tf_op jit(solution)/shard_map/attend_backward/pallas_call | solution.py:277
  455.4 74.4 %close.1 = (f32[256,1024]{1,0:T(8,128)}, f32[3072,128]{1,0:T(8,128)}, f32[48,128]{1,0:T(8,128)}) custom-call(bf16[8,256,1024]{2,1,0:T(8,128)(2,1)} %bitcast.80, bf16[256,1024]{1,0:T(8,128)(2,1)} %x_ref.5, f32[256,1024]{1,0:T(8,128)} %get-tuple-element.81.dres_ref, f32[1,1024]{1,0:T(1,128)} %get-tuple-element.96.gain_ref, ...), custom_call_target="tpu_custom_call" | custom-call | bytes 224000000 | tf_op jit(solution)/shard_map/close/pallas_call | solution.py:980
  529.9 1.1 slice.59
  530.9 1.3 slice.55
  532.2 0.7 slice_bitcast_fusion.1
  533.0 0.6 copy.52
  533.6 0.8 copy.61
  534.5 0.1 copy.49
  534.6 0.1 copy.50
  534.8 0.2 copy.48
  535.0 6.6 %convert_element_type.37 = f32[4,512,1024]{2,1,0:T(8,128)} convert(bf16[4,512,1024]{2,1,0:T(8,128)(2,1)} %get-tuple-element.90) | non-fusion elementwise | flops 2097152 | bytes 12582912 | tf_op jit(solution)/shard_map/convert_element_type | solution.py:1279
  541.6 1.3 slice_bitcast_fusion.4
  542.9 1.0 maximum_bitcast_fusion
  543.9 11.8 %convert_element_type.36 = f32[4,1024,1024]{2,1,0:T(8,128)} convert(bf16[4,1024,1024]{2,1,0:T(8,128)(2,1)} %all-reduce.2.cloned.1.call-done) | non-fusion elementwise | flops 4194304 | bytes 25165824 | tf_op jit(solution)/shard_map/convert_element_type | solution.py:1278
  555.8 0.8 copy.66
  556.6 0.0 copy-done
  556.6 1.0 copy.67
  (18 shorter events, 0.1 us)
Async XLA Ops:
  7.2 4.8 copy-start.4
  7.2 4.8 copy-start.5
  7.2 59.3 %copy-start.6 = (s32[1,2]{1,0:T(1,128)S(1)}, s32[1,2]{1,0:T(1,128)}, u32[]{:S(2)}) copy-start(s32[1,2]{1,0:T(1,128)} %param.13) | copy-start | bytes 28
  7.2 171.1 %all-gather.2.cloned.1.call-start = ((), (), s32[]{:S(2)}) async-start(), calls=%async_computation | async-start | bytes 4718592 | tf_op jit(solution)/shard_map/all_gather | solution.py:1229
  66.5 477.5 %all-reduce.2.cloned.1.call-start = ((), (), s32[]{:S(2)}) async-start(), calls=%async_computation.1 | async-start | bytes 16777216 | tf_op jit(solution)/shard_map/psum | solution.py:1254
  66.8 7.0 %copy-start.2 = (s32[2048]{0:T(1024)}, s32[2048]{0:T(1024)S(1)}, u32[]{:S(2)}) copy-start(s32[2048]{0:T(1024)S(1)} %fusion.1) | copy-start | bytes 24580
  66.8 24.9 %copy-start.3 = (bf16[8,40,128]{2,1,0:T(8,128)(2,1)S(1)}, bf16[8,40,128]{2,1,0:T(8,128)(2,1)}, u32[]{:S(2)}) copy-start(bf16[8,40,128]{2,1,0:T(8,128)(2,1)} %get-tuple-element.53) | copy-start | bytes 245764
  543.9 11.8 %copy-start.1 = (bf16[256,1024]{1,0:T(8,128)(2,1)S(1)}, bf16[256,1024]{1,0:T(8,128)(2,1)}, u32[]{:S(2)}) copy-start(bf16[256,1024]{1,0:T(8,128)(2,1)} %get-tuple-element.112) | copy-start | bytes 1572868
  543.9 12.6 %copy-start = (f32[256,1024]{1,0:T(8,128)S(1)}, f32[256,1024]{1,0:T(8,128)}, u32[]{:S(2)}) copy-start(f32[256,1024]{1,0:T(8,128)} %get-tuple-element.113) | copy-start | bytes 3145732
Sparse Core Ops, SparseCore 0:
  66.6 52.8 all-gather.1
  233.0 230.5 all-reduce.1

commit v3 on v2

--- a/solution.py
+++ b/solution.py
@@ -113,19 +113,30 @@
 
 
 def attend_backward_kernel(
-    shards, da_ref, q_ref, kv_ref, mix_ref, lse_ref, start_ref, wout_ref, w_ref, first_ref, cos_ref, sin_ref,
-    oparts_ref, residual_ref, dfirst_ref, gw_ref, gout_ref, out_ref,
+    shards, reps, experts, da_ref, q_ref, kv_ref, mix_ref, lse_ref, start_ref, wout_ref, w_ref, first_ref, cos_ref,
+    sin_ref, oparts_ref, residual_ref, gu_in, head_ref, dfirst_ref, gw_ref, gout_ref, out_ref, gu_ref,
+    copy_sem,
     keys_s, vals_s, keyt_s, dk_s, dv_s, dq_s, dqt_s, gw_s, gout_s, p_s, ds_s, *scratch
 ):
     block = pl.program_id(0)
     span = q_ref.shape[0]
     blocks = keys_s.shape[1] // span
-    fwd = Collect(shards // 2, oparts_ref, scratch)
+    fwd = Collect(shards // 2, oparts_ref, scratch[:9])
+    sums = GridSum(reps, gate_up_pieces(gu_ref, experts), scratch[9:18])
+    tick, drain = pacer(sums.steps())
+    half = gu_ref.shape[1] // 2
+    moves = [
+        pltpu.make_async_copy(head_ref.at[k], gu_ref.at[0, pl.ds(k * half, half)], copy_sem.at[k]) for k in range(2)
+    ]
 
     @pl.when(block == 0)
     def _():
-        greet_shard(shards)
+        me = lax.axis_index("shard")
+        greet([{"shard": lax.rem(me + k, shards)} for k in range(1, shards)] + Exchange.partners(reps))
         fwd.start()
+        sums.begin()
+        for move in moves:
+            move.start()
 
     lane = lax.broadcasted_iota(jnp.int32, (span, LANES), 1)
     low_lane = lane < HEAD
@@ -188,6 +199,12 @@
         turns.setdefault(0 if k == 0 else blocks - len(hops) + k, []).append(hop)
     for turn_block, some in turns.items():
         pl.when(block == turn_block)(functools.partial(fwd.carry, some))
+    for k in range(1, blocks):
+
+        @pl.when(block == k)
+        def _():
+            tick(2)
+
 
     @pl.when(block == blocks - 1)
     def _():
@@ -223,6 +240,9 @@
 
         for cut in range(2):
             fwd.finish(cut, finish_out)
+        drain()
+        for move in moves:
+            move.wait()
         fwd.settle()
 
 
@@ -264,7 +284,10 @@
     )(x, gain, w, cosine, sine, w_out, start)
 
 
-def attend_backward(d_attn, q, kv, mix, lse, start, w_out, w, first, cosine, sine, o_parts, residual, shards):
+def attend_backward(
+    d_attn, q, kv, mix, lse, start, w_out, w, first, cosine, sine, o_parts, residual, grad_gate_up, experts,
+    head_sum, shards, reps,
+):
     total, width = d_attn.shape
     span = 512 if total <= 2048 else 256
     blocks = total // span
@@ -275,17 +298,18 @@
     shape = jax.ShapeDtypeStruct
     cut = lambda a: a.reshape(blocks, span, a.shape[1])
     return pl.pallas_call(
-        functools.partial(attend_backward_kernel, shards),
+        functools.partial(attend_backward_kernel, shards, reps, experts),
         grid_spec=pltpu.PrefetchScalarGridSpec(
             num_scalar_prefetch=0,
             grid=(blocks,),
             in_specs=[
                 row(width), row(LANES), fixed((total, LANES)), col(LANES), col(2), col(1),
                 fixed(w_out.shape), fixed(w.shape), fixed((blocks, span, width)),
-                fixed((blocks, span, LANES)), fixed((blocks, span, LANES)), ANY, fixed(residual.shape),
+                fixed((blocks, span, LANES)), fixed((blocks, span, LANES)), ANY, fixed(residual.shape), ANY, ANY,
             ],
-            out_specs=[fixed((blocks, span, width)), fixed((shards, cols * width // shards // LANES, LANES)), fixed((width, LANES)), fixed(residual.shape)],
+            out_specs=[fixed((blocks, span, width)), fixed((shards, cols * width // shards // LANES, LANES)), fixed((width, LANES)), fixed(residual.shape), ANY],
             scratch_shapes=[
+                pltpu.SemaphoreType.DMA((2,)),
                 pltpu.VMEM((2, total, LANES), jnp.bfloat16),
                 pltpu.VMEM((2, total, LANES), jnp.bfloat16),
                 pltpu.VMEM((HEAD, total), jnp.bfloat16),
@@ -298,18 +322,21 @@
                 pltpu.VMEM((2, total, span), jnp.bfloat16),
                 pltpu.VMEM((2, total, span), jnp.bfloat16),
             ]
-            + Collect.boxes(shards, *residual.shape),
+            + Collect.boxes(shards, *residual.shape)
+            + GridSum.scratch(reps, 2 * len(experts), grad_gate_up.shape[1] // 2, grad_gate_up.shape[2]),
         ),
         out_shape=[
             shape((blocks, span, width), jnp.bfloat16),
             shape((shards, cols * width // shards // LANES, LANES), jnp.bfloat16),
             shape((width, LANES), jnp.bfloat16),
             shape(residual.shape, jnp.bfloat16),
+            shape(grad_gate_up.shape, jnp.bfloat16),
         ],
+        input_output_aliases={13: 4},
         compiler_params=remote_params(5, 60),
         cost_estimate=cost(34),
         name="attend_backward",
-    )(d_attn, q, kv, mix, lse, start, w_out, w, cut(first), cut(cosine), cut(sine), o_parts, residual)
+    )(d_attn, q, kv, mix, lse, start, w_out, w, cut(first), cut(cosine), cut(sine), o_parts, residual, grad_gate_up, head_sum)
 
 
 MESH = pl.DeviceIdType.MESH
@@ -677,8 +704,8 @@
 
 
 def turn_kernel(
-    shards, reps, parts_ref, gd_ref, residual_ref, cot_ref, gain_ref, gates_ref, second_ref, router_ref,
-    dres_ref, dgain_ref, drouter_ref, all_ref, gdsum_ref, dsec_s, datt_s, *scratch
+    shards, reps, parts_ref, gd_in, residual_ref, cot_ref, gain_ref, gates_ref, second_ref, router_ref,
+    dres_ref, dgain_ref, drouter_ref, all_ref, gd_ref, dsec_s, datt_s, *scratch
 ):
     me = lax.axis_index("shard")
     greet([{"shard": lax.rem(me + k, shards)} for k in range(1, shards)] + Exchange.partners(reps))
@@ -686,11 +713,10 @@
     rows, width = residual_ref.shape
     collect = Collect(chips, parts_ref, scratch[:9])
     spread = Spread(chips, datt_s, all_ref, scratch[9:14])
-    sums = GridSum(reps, [(gd_ref.at[e], gdsum_ref.at[e]) for e in range(gd_ref.shape[0])], scratch[14:23])
+    sums = GridSum(reps, [(gd_ref.at[e], gd_ref.at[e]) for e in range(gd_ref.shape[0])], scratch[14:23])
     collect.start()
     sums.begin()
-    steps = sums.steps()
-    tick = lambda: next(steps, None)
+    tick, drain = pacer(sums.steps())
     collect.carry(tick=tick)
 
     def stash(here, total):
@@ -726,8 +752,7 @@
             datt_s[here] = d_residual.astype(jnp.bfloat16)
         spread.start(cut)
     spread.carry(tick)
-    for unused in steps:
-        pass
+    drain()
     collect.settle()
     spread.settle()
 
@@ -753,6 +778,7 @@
         + Collect.boxes(shards, parts.shape[1], width)
         + Spread.sems(shards)
         + GridSum.scratch(reps, grad_down.shape[0], grad_down.shape[1], width),
+        input_output_aliases={1: 4},
         compiler_params=remote_params(3, 60),
         cost_estimate=cost(75),
         name="turn",
@@ -822,6 +848,7 @@
 
     @staticmethod
     def scratch(reps, count, rows, width):
+        count = max(count, 1)
         bits = reps.bit_length() - 1
         dma = pltpu.SemaphoreType.DMA
         return [
@@ -884,38 +911,63 @@
         lax.fori_loop(0, size // strip, body, 0)
 
     def begin(self):
-        for piece in range(len(self.pieces)):
+        loaded = [piece for piece in range(len(self.pieces)) if self.pieces[piece][0] is not None]
+        for piece in loaded:
             self.load(piece).start()
         for piece in range(len(self.pieces)):
-            self.load(piece).wait()
+            if piece in loaded:
+                self.load(piece).wait()
             self.down(piece, 0).start()
 
-    def steps(self):
-        count, bits = len(self.pieces), self.bits
-        for stage in range(bits):
-            for piece in range(count):
-                self.down(piece, stage).wait_recv()
-                self.add(piece, stage)
-                (self.down(piece, stage + 1) if stage < bits - 1 else self.up(piece, stage)).start()
-                yield
-        for stage in range(bits - 1, -1, -1):
-            for piece in range(count):
-                self.up(piece, stage, True).wait_recv()
-                (self.up(piece, stage - 1) if stage else self.store(piece)).start()
-                yield
-        for piece in range(count):
-            for stage in range(bits):
+    def sink(self, stage, piece):
+        self.down(piece, stage).wait_recv()
+        self.add(piece, stage)
+        (self.down(piece, stage + 1) if stage < self.bits - 1 else self.up(piece, stage)).start()
+
+    def rise(self, stage, piece):
+        self.up(piece, stage, True).wait_recv()
+        (self.up(piece, stage - 1) if stage else self.store(piece)).start()
+
+    def settle(self):
+        for piece in range(len(self.pieces)):
+            for stage in range(self.bits):
                 self.down(piece, stage).wait_send()
                 self.up(piece, stage).wait_send()
             self.store(piece).wait()
 
+    def steps(self):
+        order = [functools.partial(self.sink, k, p) for k in range(self.bits) for p in range(len(self.pieces))]
+        back = range(self.bits - 1, -1, -1)
+        order += [functools.partial(self.rise, k, p) for k in back for p in range(len(self.pieces))]
+        return order + [self.settle]
+
+
+def pacer(steps):
+    left = iter(steps)
+
+    def tick(count=1):
+        for unused in range(count):
+            next(left, lambda: None)()
+
+    def drain():
+        for step in left:
+            step()
+
+    return tick, drain
+
+
+def gate_up_pieces(ref, experts):
+    half = ref.shape[1] // 2
+    spots = [ref.at[e, pl.ds(k * half, half)] for e in experts for k in range(2)]
+    return [(spot, spot) for spot in spots]
+
 
 MINI = 48
 
 
 def close_kernel(
-    shards, reps, dparts_ref, x_ref, dres_ref, gain_ref, head_ref, outg_ref, drouter_ref,
-    dgain_ref, dtok_ref, share_ref, small_ref, bulk_s, mini_s, sum_s, minis_s, *scratch
+    shards, reps, experts, dparts_ref, gu_in, x_ref, dres_ref, gain_ref, head_ref, outg_ref, drouter_ref,
+    dgain_ref, dtok_ref, share_ref, small_ref, gu_ref, bulk_s, mini_s, sum_s, minis_s, *scratch
 ):
     me = lax.axis_index("shard")
     greet([{"shard": lax.rem(me + k, shards)} for k in range(1, shards)] + Exchange.partners(reps))
@@ -927,8 +979,11 @@
     mini = Direct(shards, lambda target: mini_s.at[target], lambda source: minis_s.at[source], *scratch[11:13])
     bulk_sum = Exchange(reps, bulk_s, *scratch[13:16])
     mini_sum = Exchange(reps, sum_s, *scratch[16:19])
+    sums = GridSum(reps, gate_up_pieces(gu_ref, experts), scratch[19:28])
     tok.start()
+    sums.begin()
     heads.start()
+    tick, drain = pacer(sums.steps())
     bulk_s[shards * piece :] = outg_ref[...]
     cols = gain_ref.shape[1] // shards
     mini_s[...] = jnp.zeros_like(mini_s)
@@ -936,7 +991,7 @@
         here = slice(k * cols, (k + 1) * cols)
         mini_s[k, :EXPERTS, :cols] = drouter_ref[:, here]
         mini_s[k, EXPERTS : EXPERTS + 1, :cols] = dgain_ref[:, here]
-    tok.carry()
+    tok.carry(tick=tick)
 
     def finish_tok(here, d_first):
         x = x_ref[here].astype(jnp.float32)
@@ -967,10 +1022,11 @@
         small_ref[here] = total
 
     mini_sum.run(keep_mini)
+    drain()
     tok.settle()
 
 
-def close(d_parts, x, d_residual, gain, head_parts, out_grad, d_router, d_gain, shards, reps):
+def close(d_parts, grad_gate_up, experts, x, d_residual, gain, head_parts, out_grad, d_router, d_gain, shards, reps):
     rows, width = x.shape
     shape = jax.ShapeDtypeStruct
     piece = head_parts.shape[1]
@@ -978,14 +1034,16 @@
     f32, bf16 = jnp.float32, jnp.bfloat16
     deep = lambda a: a.reshape(shards, rows, width)
     return pl.pallas_call(
-        functools.partial(close_kernel, shards, reps),
+        functools.partial(close_kernel, shards, reps, experts),
         out_shape=[
             shape((rows, width), f32),
             shape((bulk, LANES), f32),
             shape((MINI, LANES), f32),
+            shape(grad_gate_up.shape, bf16),
         ],
-        in_specs=[ANY] + [INNER] * 7,
-        out_specs=[INNER] * 3,
+        in_specs=[ANY] * 2 + [INNER] * 7,
+        out_specs=[INNER] * 3 + [ANY],
+        input_output_aliases={1: 3},
         scratch_shapes=[
             pltpu.VMEM((bulk, LANES), bf16),
             pltpu.VMEM((shards, MINI, LANES), f32),
@@ -995,11 +1053,12 @@
         + Collect.boxes(shards, rows, width)
         + Direct.sems(shards) * 2
         + Exchange.scratch(reps, bulk, bf16)
-        + Exchange.scratch(reps, MINI, f32),
+        + Exchange.scratch(reps, MINI, f32)
+        + GridSum.scratch(reps, 2 * len(experts), grad_gate_up.shape[1] // 2, width),
         compiler_params=remote_params(4, 60),
         cost_estimate=cost(70),
         name="close",
-    )(deep(d_parts), x, d_residual, gain, head_parts, out_grad, d_router, d_gain)
+    )(deep(d_parts), grad_gate_up, x, d_residual, gain, head_parts, out_grad, d_router, d_gain)
 
 
 def tn_dot(a, b):
@@ -1041,9 +1100,24 @@
         gs_ref[e, 0] = gs[e * CAP : (e + 1) * CAP]
 
 
-def expert_kernel(xs_ref, gs_ref, gate_ref, wgu_ref, wd_ref, y_ref, dy_ref, dgate_ref, ggu_ref, gd_ref, hid_s, dg_s, dgu_s):
+def expert_kernel(
+    reps, experts, xs_ref, gs_ref, gate_ref, wgu_ref, wd_ref, y_ref, dy_ref, dgate_ref, ggu_ref, gd_ref, head_ref,
+    hid_s, dg_s, dgu_s, *scratch
+):
+    expert = pl.program_id(0)
     slots = xs_ref.shape[1]
     chunk = 256
+    sums = GridSum(reps, [(None, head_ref.at[k]) for k in range(2)], scratch)
+    steps = sums.steps()
+    pl.when(expert == 0)(lambda: greet(Exchange.partners(reps)))
+    last = pl.num_programs(0) - 1
+
+    def progress(when, steps):
+        def some():
+            for step in steps:
+                step()
+
+        pl.when(when)(some)
 
     def part(i, c):
         here = pl.ds(pl.multiple_of(i * chunk, chunk), chunk)
@@ -1069,13 +1143,30 @@
         return c
 
     lax.fori_loop(0, slots // chunk, part, 0)
+    done = 0
+    if experts >= 4:
+        progress(expert == 2, steps[2:4])
+        progress(expert == 3, steps[4:6])
+        done = 6
     cols = 256
+    for k in range(xs_ref.shape[2] // cols):
+        here = slice(k * cols, (k + 1) * cols)
+        ggu_ref[0, here, :] = tn_dot(xs_ref[0, :, here], dgu_s[...]).astype(jnp.bfloat16)
+
+    @pl.when(expert == 0)
+    def _():
+        half = ggu_ref.shape[1] // 2
+        for k in range(2):
+            sums.full[k] = ggu_ref[0, k * half : (k + 1) * half]
+        sums.begin()
+
     for k in range(hid_s.shape[1] // cols):
         here = slice(k * cols, (k + 1) * cols)
         gd_ref[0, here, :] = tn_dot(hid_s[:, here], dg_s[...]).astype(jnp.bfloat16)
-    for k in range(xs_ref.shape[2] // cols):
-        here = slice(k * cols, (k + 1) * cols)
-        ggu_ref[0, here, :] = tn_dot(xs_ref[0, :, here], dgu_s[...]).astype(jnp.bfloat16)
+
+    if done:
+        progress(expert == 1, steps[:2])
+    progress(expert == last, steps[done:])
 
 
 def combine_kernel(first_ref, choice_ref, y_ref, dy_ref, dgate_ref, out_ref, dout_ref):
@@ -1100,7 +1191,7 @@
     dout_ref[0, :rows] = tn_dot(pick, dy_ref[:, 0].reshape(local * CAP, -1)).astype(jnp.bfloat16)
 
 
-def run_experts(group_in, group_cot, group_choice, router_t, w_gate_up, w_down, first_expert):
+def run_experts(group_in, group_cot, group_choice, router_t, w_gate_up, w_down, first_expert, reps):
     shards, rows, width = group_in.shape
     local = w_down.shape[0]
     slots = shards * CAP
@@ -1130,24 +1221,26 @@
     )(first_expert, group_in, group_cot, group_choice, router_t)
     flat = lambda a: a.reshape(local, slots, a.shape[3])
     each = lambda r, c: pl.BlockSpec((1, r, c), lambda e: (e, 0, 0))
-    y, dy, dgate, ggu, gd = pl.pallas_call(
-        expert_kernel,
+    y, dy, dgate, ggu, gd, head = pl.pallas_call(
+        functools.partial(expert_kernel, reps, local),
         grid=(local,),
         in_specs=[each(slots, width), each(slots, width), each(slots, 1), each(width, 2 * FF), each(FF, width)],
-        out_specs=[each(slots, width), each(slots, width), each(slots, 1), each(width, 2 * FF), each(FF, width)],
+        out_specs=[each(slots, width), each(slots, width), each(slots, 1), each(width, 2 * FF), each(FF, width), ANY],
         out_shape=[
             shape((local, slots, width), bf16),
             shape((local, slots, width), bf16),
             shape((local, slots, 1), f32),
             shape(w_gate_up.shape, bf16),
             shape(w_down.shape, bf16),
+            shape((2, width // 2, 2 * FF), bf16),
         ],
         scratch_shapes=[
             pltpu.VMEM((slots, FF), bf16),
             pltpu.VMEM((slots, width), bf16),
             pltpu.VMEM((slots, 2 * FF), bf16),
-        ],
-        compiler_params=params(60),
+        ]
+        + GridSum.scratch(reps, 2, width // 2, 2 * FF),
+        compiler_params=remote_params(6, 60),
         cost_estimate=cost(42),
         name="experts",
     )(flat(xs), flat(gs), flat(gates), w_gate_up, w_down)
@@ -1169,7 +1262,7 @@
         cost_estimate=cost(9),
         name="combine_rows",
     )(first_expert, group_choice, deep(y), deep(dy), deep(dgate))
-    return out, d_out, ggu, gd
+    return out, d_out, ggu, gd, head
 
 
 def layout(lengths, tok_index, prompt_len):
@@ -1247,20 +1340,20 @@
         group_tokens.reshape(group_len, model_width), gain_attn, w_heads, cosine, sine, own_out, start_row
     )
     residual, second_in, gates, group_in = middle(out_parts, tokens, gain_ffn, router_t, choice_t, shards)
-    out_terms, d_terms, grad_gate_up, grad_down = run_experts(
+    out_terms, d_terms, grad_gate_up, grad_down, head_sum = run_experts(
         group_in, group_cot.reshape(group_in.shape), group_choice, router_t, w_gate_up, w_down,
-        lax.axis_index("shard")[None] * w_down.shape[0],
+        lax.axis_index("shard")[None] * w_down.shape[0], reps,
     )
-    grad_gate_up = lax.psum(grad_gate_up, "rep")
     d_residual, d_gain, d_router, group_d_attn, grad_down = turn(
         d_terms, grad_down, residual, cotangent, gain_ffn, gates, second_in, router_t, shards, reps
     )
-    d_parts, head_parts, out_grad, output = attend_backward(
+    early = (1,) if group_len <= 2048 else ()
+    d_parts, head_parts, out_grad, output, grad_gate_up = attend_backward(
         group_d_attn.reshape(group_len, model_width), queries, key_values, mixed_t, log_total, start_row,
-        own_out, w_heads, group_first, cosine, sine, out_terms, residual, shards,
+        own_out, w_heads, group_first, cosine, sine, out_terms, residual, grad_gate_up, early, head_sum, shards, reps,
     )
-    d_tokens, share, small_sum = close(
-        d_parts, tokens, d_residual, gain_attn, head_parts, out_grad, d_router, d_gain, shards, reps
+    d_tokens, share, small_sum, grad_gate_up = close(
+        d_parts, grad_gate_up, tuple(range(1 + len(early), w_down.shape[0])), tokens, d_residual, gain_attn, head_parts, out_grad, d_router, d_gain, shards, reps
     )
     lines = head_parts.shape[1]
     head_grads = share[: shards * lines].reshape(shards, lines, LANES // own_rows, own_rows)

time: 573 us -> 594 us (1.037)
  Pallas kernels: 509 us -> 534 us
    pallas_call x3, Pallas kernels: 171 us -> 250 us  [the longest x1 105 us: close(): pl.pallas_call(functools.partial(close_kernel, shards, reps, experts), ou...]
    pallas_call x1, Pallas kernels: 154 us -> 102 us  [turn(): pl.pallas_call(functools.partial(turn_kernel, shards, reps), out_shape=[s...]
  transfers between devices with their start and end apart: 2 -> 1, of which waited for: 0 -> 0; matrix products, arithmetic and copies ran while one was open for 4% -> 1% of each run, Pallas kernels for 71% -> 18%
where the time goes in v3:
time: 594 us; the launch traced here: 590 us
  Pallas kernels  534 us (90%)
  other arithmetic  28.3 us (5%)
  between operations  14.5 us (2%)
  local copies, waits for them, and re-layouts  12.5 us (2%)
    pallas_call x1, Pallas kernels, close(): pl.pallas_call(functools.partial(close_kernel, shards, reps, experts), ou...  105 us
    pallas_call x1, Pallas kernels, turn(): pl.pallas_call(functools.partial(turn_kernel, shards, reps), out_shape=[s...  102 us
    pallas_call x1, Pallas kernels, middle(): pl.pallas_call(functools.partial(middle_kernel, shards), out_shape=[shape...  85.8 us
    pallas_call x1, Pallas kernels, attend_backward(): pl.pallas_call(functools.partial(attend_backward_kernel, shards, reps, ex...  85.5 us
    pallas_call x1, Pallas kernels, run_experts(): pl.pallas_call(functools.partial(expert_kernel, reps, local), grid=(local...  59.6 us
    pallas_call x1, Pallas kernels, open_gathers(): pl.pallas_call(functools.partial(open_kernel, shards), out_shape=[wide(x)...  53.8 us
    pallas_call x1, Pallas kernels, attend_forward(): pl.pallas_call(attend_forward_kernel, grid_spec=pltpu.PrefetchScalarGridS...  17.9 us
    pallas_call x1, Pallas kernels, run_experts(): pl.pallas_call(pick_kernel, grid_spec=pltpu.PrefetchScalarGridSpec(num_sc...  13 us
  transfers between devices with their start and end apart: 1, of which 0 were waited for; matrix products, arithmetic and copies ran while one was open for 1% of the time, Pallas kernels for 18%

profile of v3, /device:TPU:0, one launch (start us, length us, event | category | flops | bytes accessed | tf_op | source)
XLA Modules:
  0.0 589.5 jit_solution(624024026077242302)
XLA Ops:
  7.2 0.0 copy-start.4
  7.2 0.0 copy-start.5
  7.2 0.0 copy-start.6
  7.2 0.0 all-gather.2.cloned.1.call-start
  7.3 1.0 slice.47
  8.2 1.0 fusion.10
  9.2 0.7 copy.65
  9.9 0.2 copy.56
  10.1 0.2 copy.47
  10.3 0.1 copy.57
  10.4 0.2 copy.48
  10.6 0.1 copy.58
  10.7 0.2 copy.49
  10.9 0.1 pad.9.clone
  11.0 1.0 maximum_bitcast_fusion.1.piece_ref
  12.0 0.0 copy-done.4
  12.0 0.7 maximum_maximum_fusion.small_ref
  12.7 53.8 %open_gathers.1 = (bf16[8,256,1024]{2,1,0:T(8,128)(2,1)}, bf16[8,40,128]{2,1,0:T(8,128)(2,1)}, s32[8,8,256]{2,1,0:T(8,128)}, bf16[8,128,256]{2,1,0:T(8,128)(2,1)}) custom-call(bf16[256,1024]{1,0:T(8,128)(2,1)} %x_ref.5, bf16[40,128]{1,0:T(8,128)(2,1)} %maximum_maximum_fusion.small_ref, s32[8,256]{1,0:T(8,128)} %bitcast.102, ...), custom_call_target="tpu_custom_call" | custom-call | bytes 144000000 | tf_op jit(solution)/shard_map/open_gathers/pallas_call | solution.py:632
  66.4 0.0 all-gather.2.cloned.1.call-update
  66.5 0.1 fusion.4
  66.6 0.1 fusion.1
  66.7 0.0 copy-start.2
  66.8 5.6 fusion
  72.3 1.4 fusion.2
  73.7 17.9 %attend_forward.1 = (bf16[2048,1024]{1,0:T(8,128)(2,1)}, bf16[2048,1024]{1,0:T(8,128)(2,1)}, bf16[2048,128]{1,0:T(8,128)(2,1)}, bf16[2048,128]{1,0:T(8,128)(2,1)...) custom-call(bf16[2048,1024]{1,0:T(8,128)(2,1)} %bitcast.82, f32[1,1024]{1,0:T(1,128)} %get-tuple-element.102.gain_ref, ...), custom_call_target="tpu_custom_call" | custom-call | bytes 54400000 | tf_op jit(solution)/shard_map/attend_forward/pallas_call | solution.py:257
  91.6 0.6 copy_bitcast_fusion.1.router_ref
  92.3 85.8 %middle.1 = (f32[256,1024]{1,0:T(8,128)}, bf16[256,1024]{1,0:T(8,128)(2,1)}, f32[32,256]{1,0:T(8,128)}, bf16[8,256,1024]{2,1,0:T(8,128)(2,1)}) custom-call(bf16[8,256,1024]{2,1,0:T(8,128)(2,1)} %bitcast.83, bf16[256,1024]{1,0:T(8,128)(2,1)} %x_ref.5, f32[1,1024]{1,0:T(1,128)} %get-tuple-element.101.gain_ref, bf16[32,1024]{1,0:T(8,128)(2,1)} %copy_bitcast_fusion.1.router_ref, ...), custom_call_target="tpu_custom_call" | custom-call | bytes 240000000 | tf_op jit(solution)/shard_map/middle/pallas_call | solution.py:689
  178.1 0.0 all-gather.2.cloned.1.call-done
  178.1 13.0 %pick_rows.1 = (bf16[4,8,96,1024]{3,2,1,0:T(8,128)(2,1)}, bf16[4,8,96,1024]{3,2,1,0:T(8,128)(2,1)}, f32[4,8,96,1]{3,2,1,0:T(8,128)}) custom-call(s32[1]{0:T(128)} %bitcast.first_ref, bf16[8,256,1024]{2,1,0:T(8,128)(2,1)} %get-tuple-element.62.x_ref, bf16[8,256,1024]{2,1,0:T(8,128)(2,1)} %bitcast.81, s32[8,8,256]{2,1,0:T(8,128)} %get-tuple-element.53.choice_ref, ...), custom_call_target="tpu_custom_call" | custom-call | bytes 25600000 | tf_op jit(solution)/shard_map/pick_rows/pallas_call | solution.py:1205
  191.1 59.6 %experts.1 = (bf16[4,768,1024]{2,1,0:T(8,128)(2,1)}, bf16[4,768,1024]{2,1,0:T(8,128)(2,1)}, f32[4,768,1]{2,1,0:T(8,128)}, bf16[4,1024,1024]{2,1,0:T(8,128)(2,1)}...) custom-call(bf16[4,768,1024]{2,1,0:T(8,128)(2,1)} %bitcast.76, bf16[4,768,1024]{2,1,0:T(8,128)(2,1)} %bitcast.77, ...), custom_call_target="tpu_custom_call" | custom-call | bytes 134400000 | tf_op jit(solution)/shard_map/experts/pallas_call | solution.py:1224
  250.7 12.1 %combine_rows.1 = (bf16[8,256,1024]{2,1,0:T(8,128)(2,1)}, bf16[8,272,1024]{2,1,0:T(8,128)(2,1)}) custom-call(s32[1]{0:T(128)} %bitcast.first_ref, s32[8,8,256]{2,1,0:T(8,128)} %get-tuple-element.53.choice_ref, bf16[4,8,96,1024]{3,2,1,0:T(8,128)(2,1)} %bitcast.74, bf16[4,8,96,1024]{3,2,1,0:T(8,128)(2,1)} %bitcast.75, f32[4,8,96,1]{3,2,1,0:T(8,128)} %bitcast.91), custom_call_target="tpu_custom_call" | custom-call | bytes 28800000 | tf_op jit(solution)/shard_map/combine_rows/pallas_call | solution.py:1249
  262.8 101.5 %turn.1 = (f32[256,1024]{1,0:T(8,128)}, f32[1,1024]{1,0:T(1,128)}, f32[32,1024]{1,0:T(8,128)}, bf16[8,256,1024]{2,1,0:T(8,128)(2,1)}, bf16[4,512,1024]{2,1,0:T(8,128)(2,1)}) custom-call(bf16[8,272,1024]{2,1,0:T(8,128)(2,1)} %get-tuple-element.70.parts_ref, bf16[4,512,1024]{2,1,0:T(8,128)(2,1)} %get-tuple-element.71.gd_in, ...), custom_call_target="tpu_custom_call", output_to_operand_aliasing={{4}: (1, {})} | custom-call | bytes 240000000 | tf_op jit(solution)/shard_map/turn/pallas_call | solution.py:763
  364.3 85.5 %attend_backward.1 = (bf16[4,512,1024]{2,1,0:T(8,128)(2,1)}, bf16[8,256,128]{2,1,0:T(8,128)(2,1)}, bf16[1024,128]{1,0:T(8,128)(2,1)}, bf16[256,1024]{1,0:T(8,128)(2,1)}, bf16[4,1024,1024]{2,1,0:T(8,128)(2,1)}) custom-call(bf16[2048,1024]{1,0:T(8,128)(2,1)} %bitcast.79, bf16[2048,128]{1,0:T(8,128)(2,1)} %get-tuple-element.76.q_ref, ...), custom_call_target="tpu_custom_call", output_to_operand_aliasing={{4}: (13, {})} | custom-call | bytes 108800000 | tf_op jit(solution)/shard_map/attend_backward/pallas_call | solution.py:300
  449.9 104.9 %close.1 = (f32[256,1024]{1,0:T(8,128)}, f32[3072,128]{1,0:T(8,128)}, f32[48,128]{1,0:T(8,128)}, bf16[4,1024,1024]{2,1,0:T(8,128)(2,1)}) custom-call(bf16[8,256,1024]{2,1,0:T(8,128)(2,1)} %bitcast.80, bf16[4,1024,1024]{2,1,0:T(8,128)(2,1)} %get-tuple-element.86.gu_in, bf16[256,1024]{1,0:T(8,128)(2,1)} %x_ref.5, ...), custom_call_target="tpu_custom_call", output_to_operand_aliasing={{3}: (1, {})} | custom-call | bytes 224000000 | tf_op jit(solution)/shard_map/close/pallas_call | solution.py:1036
  554.8 1.3 slice_bitcast_fusion.4
  556.1 0.7 slice_bitcast_fusion.1
  556.8 1.1 slice.59
  557.9 1.3 slice.55
  559.2 0.6 copy.55
  559.9 0.8 copy.64
  560.7 0.1 copy.52
  560.8 0.1 copy.53
  561.0 0.2 copy.51
  561.2 6.6 %convert_element_type.37 = f32[4,512,1024]{2,1,0:T(8,128)} convert(bf16[4,512,1024]{2,1,0:T(8,128)(2,1)} %get-tuple-element.96) | non-fusion elementwise | flops 2097152 | bytes 12582912 | tf_op jit(solution)/shard_map/convert_element_type | solution.py:1372
  567.8 11.8 %convert_element_type.36 = f32[4,1024,1024]{2,1,0:T(8,128)} convert(bf16[4,1024,1024]{2,1,0:T(8,128)(2,1)} %get-tuple-element.95) | non-fusion elementwise | flops 4194304 | bytes 25165824 | tf_op jit(solution)/shard_map/convert_element_type | solution.py:1371
  579.6 1.0 maximum_bitcast_fusion
  580.7 0.8 copy.71
  581.5 1.0 copy.72
  (15 shorter events, 0.1 us)
Async XLA Ops:
  7.2 4.8 copy-start.4
  7.2 4.8 copy-start.5
  7.2 59.3 %copy-start.6 = (s32[1,2]{1,0:T(1,128)S(1)}, s32[1,2]{1,0:T(1,128)}, u32[]{:S(2)}) copy-start(s32[1,2]{1,0:T(1,128)} %param.13) | copy-start | bytes 28
  7.2 170.9 %all-gather.2.cloned.1.call-start = ((), (), s32[]{:S(2)}) async-start(), calls=%async_computation | async-start | bytes 4718592 | tf_op jit(solution)/shard_map/all_gather | solution.py:1322
  66.7 7.0 %copy-start.2 = (s32[2048]{0:T(1024)}, s32[2048]{0:T(1024)S(1)}, u32[]{:S(2)}) copy-start(s32[2048]{0:T(1024)S(1)} %fusion.1) | copy-start | bytes 24580
  66.7 24.9 %copy-start.3 = (bf16[8,40,128]{2,1,0:T(8,128)(2,1)S(1)}, bf16[8,40,128]{2,1,0:T(8,128)(2,1)}, u32[]{:S(2)}) copy-start(bf16[8,40,128]{2,1,0:T(8,128)(2,1)} %get-tuple-element.56) | copy-start | bytes 245764
  567.8 12.9 %copy-start.1 = (bf16[256,1024]{1,0:T(8,128)(2,1)S(1)}, bf16[256,1024]{1,0:T(8,128)(2,1)}, u32[]{:S(2)}) copy-start(bf16[256,1024]{1,0:T(8,128)(2,1)} %get-tuple-element.118) | copy-start | bytes 1572868
  567.8 13.7 %copy-start = (f32[256,1024]{1,0:T(8,128)S(1)}, f32[256,1024]{1,0:T(8,128)}, u32[]{:S(2)}) copy-start(f32[256,1024]{1,0:T(8,128)} %get-tuple-element.119) | copy-start | bytes 3145732
Sparse Core Ops, SparseCore 0:
  66.6 52.9 all-gather.1
